TPU v7x, 32 devices: a whole 2x2x4 slice. The times are simulated.
32 devices in a mesh: ens: 4 (over y, core), space: 8 (over z, x).
Axes of the slice: x: 2, y: 2, z: 4, core: 2. Of those that a mesh axis runs over, the one named last changes fastest.
Arguments:
- prior_profiles: bfloat16 [128, 64, 64, 128], P('ens', 'space'), may hold values from -6 to 6
- conductivity_profile: bfloat16 [128, 64, 64, 128], P('ens', 'space'), may hold values from 0.5 to 2
- sensor_position_flat: int32 [8192], P('space'), may hold values from 0 to 65535
- observation_slot_count: int32 [8], P('space'), may hold values from 1 to 1024, 5120 in all
- obs_values: float32 [8192], P('space'), may hold values from -6 to 6
- obs_std: float32 [8192], P('space'), may hold values from 0.3 to 3
- obs_noise: float32 [128, 8192], P('ens', 'space'), may hold values from -6 to 6
- params: float32 [128, 2048], P('ens', 'space'), may hold values from -6 to 6
Outputs:
- posterior_parameters: float32 [128, 2048], P('ens', 'space')
- predicted_states: float32 [128, 64, 64, 128], P('ens', 'space')
Inputs may be any that keep to these rules, and one draw needn't show every extreme that they name: The live slots of a slab are its first observation_slot_count ones.
All inputs are finite; a program needn't handle non-finite values. No bound on the sum of `observation_slot_count` on one device may be relied on, other than what follows from the above.
Results may differ from a plain program's by a relative error of at most 0.0003.
Values may be sent and summed in bfloat16 or wider, within the bound.
A program may use at most 256 MiB of HBM per device.

v0:
```python
import math

import jax
import jax.numpy as jnp
from jax import lax
from jax.sharding import PartitionSpec as P

step_size = 0.08


def extended(cells, sides, width):
    for axis, dim in sides:
        count = lax.axis_size(axis)
        ends = count - 1
        head = lax.slice_in_dim(cells, 0, width, axis=dim)
        tail = lax.slice_in_dim(cells, cells.shape[dim] - width, cells.shape[dim], axis=dim)
        cells = jnp.concatenate(
            [
                lax.ppermute(tail, axis, [(i, (i + 1) % count) for i in range(ends)]),
                cells,
                lax.ppermute(head, axis, [((i + 1) % count, i) for i in range(ends)]),
            ],
            axis=dim,
        )
    return cells


def inner_window(array, starts):
    for dimension in range(3):
        which_axis = array.ndim - 3 + dimension
        extent = array.shape[which_axis] - 2
        array = lax.slice_in_dim(
            array, starts[dimension], starts[dimension] + extent, axis=which_axis
        )
    return array


def spread_heat_onestep(field, coeff):
    centre_u = inner_window(field, (1, 1, 1))
    centre_k = inner_window(coeff, (1, 1, 1))
    flux = jnp.zeros_like(centre_u)
    for dimension in range(3):
        for offset in (0, 2):
            starts = [1, 1, 1]
            starts[dimension] = offset
            neigh_u = inner_window(field, tuple(starts))
            neigh_k = inner_window(coeff, tuple(starts))
            flux = flux + 0.5 * (centre_k + neigh_k) * (neigh_u - centre_u)
    return centre_u + step_size * flux


def shards(
    prior_profiles,
    conductivity_profile,
    sensor_position_flat,
    observation_slot_count,
    obs_values,
    obs_std,
    obs_noise,
    params,
):
    stacked = jnp.stack([prior_profiles, conductivity_profile])
    bordered_profile = extended(stacked, (("space", 2),), 1)
    bordered_profile = jnp.pad(
        bordered_profile.astype(jnp.float32), ((0, 0), (0, 0), (0, 0), (1, 1), (1, 1))
    )
    predicted_states = spread_heat_onestep(bordered_profile[0], bordered_profile[1])
    resident_realizations = predicted_states.shape[0]
    sampled_readings = jnp.take(
        predicted_states.reshape(resident_realizations, -1), sensor_position_flat, axis=1
    )
    live_slots = (
        jnp.arange(sensor_position_flat.shape[0], dtype=jnp.int32) < observation_slot_count[0]
    )
    ensemble = resident_realizations * lax.axis_size("ens")
    ens_scale = math.sqrt(ensemble - 1.0)
    ens_rank = lax.axis_index("ens")
    all_picked, all_noise = (
        lax.all_gather(sampled_readings, "ens", axis=0, tiled=True),
        lax.all_gather(obs_noise, "ens", axis=0, tiled=True),
    )
    centre = jnp.mean(all_picked, axis=0)
    spread = jnp.where(live_slots, (all_picked - centre) / (obs_std * ens_scale), 0.0)
    misfit = jnp.where(live_slots, (obs_values - all_picked) / obs_std + all_noise, 0.0)
    cross_part = jnp.dot(spread, misfit.T, precision=lax.Precision.HIGHEST)
    gram_matrix = jnp.dot(spread, spread.T, precision=lax.Precision.HIGHEST)
    gram_matrix, cross_part = lax.psum((gram_matrix, cross_part), "space")
    factor = jnp.linalg.cholesky(gram_matrix + jnp.eye(ensemble, dtype=jnp.float32))
    solved = jax.scipy.linalg.cho_solve((factor, True), cross_part)
    all_params = lax.all_gather(params, "ens", axis=0, tiled=True)
    anomaly = (all_params - jnp.mean(all_params, axis=0)) / ens_scale
    own_weights = lax.dynamic_slice_in_dim(
        solved, ens_rank * resident_realizations, resident_realizations, 1
    )
    posterior_parameters = params + jnp.dot(own_weights.T, anomaly, precision=lax.Precision.HIGHEST)
    return (posterior_parameters, predicted_states)


def solution(mesh):
    in_specs = (
        P("ens", "space", None, None),
        P("ens", "space", None, None),
        P("space"),
        P("space"),
        P("space"),
        P("space"),
        P("ens", "space"),
        P("ens", "space"),
    )
    out_specs = (P("ens", "space"), P("ens", "space", None, None))
    return jax.shard_map(shards, mesh=mesh, in_specs=in_specs, out_specs=out_specs, check_vma=False)
```

profile of v0, /device:TPU:0, one launch (start us, length us, event | category | flops | bytes accessed | tf_op | source)
XLA Modules:
  0.0 345.3 jit_solution(18058105342127222573)
XLA Ops:
  7.2 0.0 copy-start.1
  7.2 0.0 copy-start
  7.2 0.0 copy-start.2
  7.2 0.0 copy-start.3
  7.2 0.0 all-reduce.4.cloned.1.call-start
  7.2 3.1 pad_maximum_fusion.1
  10.3 4.9 %collective-permute-start = (bf16[2,32,1,64,128]{4,3,2,1,0:T(8,128)(2,1)}, bf16[2,32,1,64,128]{4,3,2,1,0:T(8,128)(2,1)S(1)}, u32[]{:S(2)}, u32[]{:S(2)}) collective-permute-start(bf16[2,32,1,64,128]{4,3,2,1,0:T(8,128)(2,1)} %get-tuple-element.6), channel_id=1, source_target_pairs={{0,1},{1,2},{2,3},{3,4},{4,5},{5,6},{6,7},{8,9},{9,10},{10,11},{11... | collective-permute-start | bytes 3145736 | tf_op jit(solution)/shard_map/ppermute | solution.py:19
  15.3 1.3 collective-permute-start.1
  17.2 0.0 copy-done.1
  17.2 5.4 %all_gather.11 = f32[128,256]{1,0:T(8,128)S(1)} all-gather(f32[32,256]{1,0:T(8,128)S(1)} %copy-done.1), channel_id=1, replica_groups=mesh['ens'=4,'space'=8] {'ens'}, dimensions={0}, use_global_device_ids=true | all-gather | bytes 163840 | tf_op jit(solution)/shard_map/all_gather | solution.py:90
  22.7 0.0 copy-done
  22.7 7.3 %all_gather.10 = f32[128,1024]{1,0:T(8,128)S(1)} all-gather(f32[32,1024]{1,0:T(8,128)S(1)} %copy-done), channel_id=1, replica_groups=mesh['ens'=4,'space'=8] {'ens'}, dimensions={0}, use_global_device_ids=true | all-gather | bytes 655360 | tf_op jit(solution)/shard_map/all_gather | solution.py:80
  30.0 0.0 copy-done.2
  30.0 0.0 copy-done.3
  30.0 30.4 %collective-permute-done = bf16[2,32,1,64,128]{4,3,2,1,0:T(8,128)(2,1)S(1)} collective-permute-done((bf16[2,32,1,64,128]{4,3,2,1,0:T(8,128)(2,1)}, bf16[2,32,1,64,128]{4,3,2,1,0:T(8,128)(2,1)S(1)}, u32[]{:S(2)}, u32[]{:S(2)}) %collective-permute-start) | collective-permute-done | bytes 1048608 | tf_op jit(solution)/shard_map/ppermute | solution.py:19
  60.4 0.0 collective-permute-done.1
  60.4 24.4 %fusion.3 = f32[2,32,10,66,130]{4,3,2,1,0:T(8,128)} fusion(bf16[2,32,1,64,128]{4,3,2,1,0:T(8,128)(2,1)S(1)} %collective-permute-done.1, bf16[2,32,1,64,128]{4,3,2,1,0:T(8,128)(2,1)S(1)} %collective-permute-done, bf16[1,32,8,64,128]{4,3,2,1,0:T(8,128)(2,1)} %bitcast.26, bf16[1,32,8,64,128]{4,3,2,1,0:T(8,128)(2,1)} %bitcast.28), kind=kLoop, calls=%fused_computation.11 | loop fusion | flops 126297600 | bytes 32450560 | tf_op jit(solution)/shard_map/jit(_pad)/pad | solution.py:64
  84.7 31.1 %slice_bitcast_fusion = (f32[32,10,66,130]{3,2,1,0:T(8,128)}, f32[32,10,66,130]{3,2,1,0:T(8,128)}) fusion(f32[2,32,10,66,130]{4,3,2,1,0:T(8,128)} %fusion.3), kind=kLoop, calls=%fused_computation.8 | loop fusion | bytes 43929600 | tf_op jit(solution)/shard_map/squeeze | solution.py:67
  115.9 79.3 %fusion.12 = f32[32,8,64,128]{3,2,1,0:T(8,128)} fusion(f32[32,10,66,130]{3,2,1,0:T(8,128)} %get-tuple-element.5, f32[32,10,66,130]{3,2,1,0:T(8,128)} %get-tuple-element.4), kind=kLoop, calls=%fused_computation.22 | loop fusion | flops 65011712 | bytes 125829120 | tf_op jit(solution)/shard_map/add | solution.py:49
  195.2 0.0 copy-start.4
  195.2 19.8 %copy.13 = f32[32,8,64,128]{0,3,2,1:T(8,128)} copy(f32[32,8,64,128]{3,2,1,0:T(8,128)} %fusion.12) | data formatting | bytes 16777216 | tf_op jit(solution)/shard_map/add | solution.py:49
  215.0 13.3 %gather_fusion = f32[1024,32]{1,0:T(8,128)S(1)} fusion(f32[32,65536]{0,1:T(8,128)} %bitcast.24, s32[1024]{0:T(1024)S(1)} %fusion.55), kind=kCustom, calls=%fused_computation | custom fusion | bytes 266240 | tf_op jit(solution)/shard_map/jit(_take)/gather | solution.py:69
  228.3 0.2 select_bitcast_fusion
  228.5 0.2 copy.14
  228.7 7.4 %all_gather.9 = f32[128,1024]{1,0:T(8,128)S(1)} all-gather(f32[32,1024]{1,0:T(8,128)S(1)} %copy.14), channel_id=1, replica_groups=mesh['ens'=4,'space'=8] {'ens'}, dimensions={0}, use_global_device_ids=true | all-gather | bytes 655360 | tf_op jit(solution)/shard_map/all_gather | solution.py:79
  236.1 1.3 fusion.33
  237.4 0.0 copy-done.4
  237.4 1.3 fusion.28
  238.7 0.0 all-reduce.4.cloned.1.call-update
  238.8 72.7 %all-reduce.4.cloned.1.call-done = (f32[128,128]{1,0:T(8,128)}, f32[128,128]{1,0:T(8,128)}) async-done(((f32[128,128]{1,0:T(8,128)}, f32[128,128]{1,0:T(8,128)}), (f32[128,128]{1,0:T(8,128)}, f32[128,128]{1,0:T(8,128)})) %all-reduce.4.cloned.1.call-update) | async-done | bytes 131088 | tf_op jit(solution)/shard_map/psum | solution.py:87
  311.5 0.9 convert_add_fusion
  312.3 0.1 copy.15
  312.4 0.9 fusion.51
  313.3 11.7 %cholesky.17 = f32[128,128]{1,0:T(8,128)S(1)} custom-call(f32[128,128]{1,0:T(8,128)S(1)} %fusion.51), custom_call_target="Cholesky" | custom-call | tf_op jit(solution)/shard_map/jit(cholesky)/cholesky | solution.py:88
  325.0 0.6 compare_reduce_fusion
  325.7 0.7 fusion.46
  326.3 9.8 %custom-call.10 = f32[1,128,128]{1,2,0:T(8,128)S(1)} custom-call(f32[1,128,128]{2,1,0:T(8,128)S(1)} %fusion.46), custom_call_target="InvertDiagBlocksLowerTriangular" | custom-call | tf_op jit(solution)/shard_map/jit(_cho_solve)/triangular_solve | solution.py:89
  336.1 1.1 fusion.49
  337.3 0.2 fusion.47
  337.5 1.0 convolution_add_fusion
  (9 shorter events, 0.1 us)
Async XLA Ops:
  7.2 10.0 %copy-start.1 = (f32[32,256]{1,0:T(8,128)S(1)}, f32[32,256]{1,0:T(8,128)}, u32[]{:S(2)}) copy-start(f32[32,256]{1,0:T(8,128)} %param.15) | copy-start | bytes 98308
  7.2 15.5 %copy-start = (f32[32,1024]{1,0:T(8,128)S(1)}, f32[32,1024]{1,0:T(8,128)}, u32[]{:S(2)}) copy-start(f32[32,1024]{1,0:T(8,128)} %param.14) | copy-start | bytes 393220
  7.2 22.8 %copy-start.2 = (s32[1024]{0:T(1024)S(1)}, s32[1024]{0:T(1024)}, u32[]{:S(2)}) copy-start(s32[1024]{0:T(1024)} %param.10) | copy-start | bytes 12292
  7.2 22.8 %copy-start.3 = (f32[1024]{0:T(1024)S(1)}, f32[1024]{0:T(1024)}, u32[]{:S(2)}) copy-start(f32[1024]{0:T(1024)} %param.13) | copy-start | bytes 12292
  7.2 304.3 %all-reduce.4.cloned.1.call-start = ((), (), s32[]{:S(2)}) async-start(), calls=%async_computation | async-start | bytes 262144 | tf_op jit(solution)/shard_map/psum | solution.py:87
  10.3 50.1 %collective-permute-start = (bf16[2,32,1,64,128]{4,3,2,1,0:T(8,128)(2,1)}, bf16[2,32,1,64,128]{4,3,2,1,0:T(8,128)(2,1)S(1)}, u32[]{:S(2)}, u32[]{:S(2)}) collective-permute-start(bf16[2,32,1,64,128]{4,3,2,1,0:T(8,128)(2,1)} %get-tuple-element.6), channel_id=1, source_target_pairs={{0,1},{1,2},{2,3},{3,4},{4,5},{5,6},{6,7},{8,9},{9,10},{10,11},{11... | collective-permute-start | bytes 3145736 | tf_op jit(solution)/shard_map/ppermute | solution.py:19
  15.3 45.1 %collective-permute-start.1 = (bf16[2,32,1,64,128]{4,3,2,1,0:T(8,128)(2,1)}, bf16[2,32,1,64,128]{4,3,2,1,0:T(8,128)(2,1)S(1)}, u32[]{:S(2)}, u32[]{:S(2)}) collective-permute-start(bf16[2,32,1,64,128]{4,3,2,1,0:T(8,128)(2,1)} %get-tuple-element.7), channel_id=1, source_target_pairs={{1,0},{2,1},{3,2},{4,3},{5,4},{6,5},{7,6},{9,8},{10,9},{11,10},{12... | collective-permute-start | bytes 3145736 | tf_op jit(solution)/shard_map/ppermute | solution.py:21
  195.2 42.3 %copy-start.4 = (f32[1024]{0:T(1024)S(1)}, f32[1024]{0:T(1024)}, u32[]{:S(2)}) copy-start(f32[1024]{0:T(1024)} %param.12) | copy-start | bytes 12292
Sparse Core Ops, SparseCore 0:
  238.9 72.5 all-reduce.3
where the time goes:
time: 346 us; the launch traced here: 345 us
  other arithmetic  132 us (38%)
  waiting for transfers between devices  103 us (30%)
  local copies, waits for them, and re-layouts  64.6 us (19%)
  blocking collectives  20.1 us (6%)
  between operations  14.9 us (4%)
  starting transfers between devices  6.25 us (2%)
  matrix products  4.87 us (1%)
    add x1, other arithmetic, spread_heat_onestep(): return centre_u + step_size * flux  79.3 us
    psum x1, waiting for transfers between devices, shards(): gram_matrix, cross_part = lax.psum((gram_matrix, cross_part), 'space')  72.7 us
    squeeze x1, local copies, waits for them, and re-layouts, shards(): bordered_profile[1]  31.1 us
    ppermute x1, waiting for transfers between devices, extended(): lax.ppermute(tail, axis, [(i, (i + 1) % count) for i in range(ends)])  30.4 us
    pad x1, other arithmetic, shards(): jnp.pad(bordered_profile.astype(jnp.float32), ((0, 0), (0, 0), (0, 0), (1...  24.4 us
    add x1, local copies, waits for them, and re-layouts, spread_heat_onestep(): return centre_u + step_size * flux  19.8 us
    gather x1, local copies, waits for them, and re-layouts, shards(): jnp.take(predicted_states.reshape(resident_realizations, -1), sensor_posi...  13.3 us
    another operation x3, other arithmetic, shards(): jnp.linalg.cholesky(gram_matrix + jnp.eye(ensemble, dtype=jnp.float32))  12.4 us
  transfers between devices with their start and end apart: 3, of which 2 were waited for; matrix products, arithmetic and copies ran while one was open for 0% of the time, Pallas kernels for 0%

commit v1 on v0

v1 whole, which is shorter than its diff:
```python
import functools
import math

import jax
import jax.numpy as jnp
from jax import lax
from jax.experimental import pallas as pl
from jax.experimental.pallas import tpu as pltpu
from jax.sharding import PartitionSpec as P

half_step = 0.04
HI = lax.Precision.HIGHEST
MESH = pl.DeviceIdType.MESH


def stencil_kernel(u_ref, k_ref, o_ref):
    members, cz, nx, ny = u_ref.shape
    row = lax.broadcasted_iota(jnp.int32, (nx, ny), 0)
    lane = lax.broadcasted_iota(jnp.int32, (nx, ny), 1)
    first_x, last_x = row == 0, row == nx - 1
    first_y, last_y = lane == 0, lane == ny - 1

    def member(m, carry):
        below = None
        u = u_ref[m, 0].astype(jnp.float32)
        k = k_ref[m, 0].astype(jnp.float32)
        for z in range(cz):
            ku = k * u
            fx = (k + pltpu.roll(k, nx - 1, 0)) * (pltpu.roll(u, nx - 1, 0) - u)
            total = jnp.where(last_x, -ku, fx) - jnp.where(first_x, ku, pltpu.roll(fx, 1, 0))
            fy = (k + pltpu.roll(k, ny - 1, 1)) * (pltpu.roll(u, ny - 1, 1) - u)
            total += jnp.where(last_y, -ku, fy) - jnp.where(first_y, ku, pltpu.roll(fy, 1, 1))
            if below is not None:
                total -= below
            if z < cz - 1:
                u_next = u_ref[m, z + 1].astype(jnp.float32)
                k_next = k_ref[m, z + 1].astype(jnp.float32)
                below = (k + k_next) * (u_next - u)
                total += below
            o_ref[m, z] = u + half_step * total
            if z < cz - 1:
                u, k = u_next, k_next
        return carry

    lax.fori_loop(0, members, member, 0)


def stencil(u, k):
    m, cz, nx, ny = u.shape
    block = 4
    spec = pl.BlockSpec((block, cz, nx, ny), lambda g: (g, 0, 0, 0))
    return pl.pallas_call(
        stencil_kernel,
        grid=(m // block,),
        in_specs=[spec, spec],
        out_specs=spec,
        out_shape=jax.ShapeDtypeStruct(u.shape, jnp.float32),
        cost_estimate=pl.CostEstimate(
            flops=40 * u.size, bytes_accessed=8 * u.size, transcendentals=0
        ),
        name="stencil",
    )(u, k)


def border_kernel(
    row_ref, col_ref, p_ref, u_ref, k_ref, ulo_ref, klo_ref, uhi_ref, khi_ref,
    o_ref, picked_ref, scr,
):
    g, e = pl.program_id(0), pl.program_id(1)
    block, cz, nx, ny = p_ref.shape
    cells = cz * nx
    members = scr.shape[0] // cells
    base = g * block
    u = u_ref[:, 0].astype(jnp.float32)
    k = k_ref[:, 0].astype(jnp.float32)

    def fix(z, un_ref, kn_ref):
        un = un_ref[...].astype(jnp.float32)
        kn = kn_ref[...].astype(jnp.float32)
        new = p_ref[:, z] + half_step * (k + kn) * (un - u)
        o_ref[:, 0] = new
        for b in range(block):
            start = pl.multiple_of((base + b) * cells + z * nx, nx)
            scr[pl.ds(start, nx), :] = new[b]

    @pl.when(e == 0)
    def _():
        fix(0, ulo_ref, klo_ref)
        for b in range(block):
            for z in range(1, cz - 1):
                start = pl.multiple_of((base + b) * cells + z * nx, nx)
                scr[pl.ds(start, nx), :] = p_ref[b, z]

    @pl.when(e == 1)
    def _():
        fix(cz - 1, uhi_ref, khi_ref)

    @pl.when(jnp.logical_and(g == pl.num_programs(0) - 1, e == 1))
    def _():
        lane = lax.broadcasted_iota(jnp.int32, (8, ny), 1)
        groups = members // 8
        unroll = 8

        def chunk(c, carry):
            def step(s, acc):
                acc = list(acc)
                for i in range(unroll):
                    jj = s * unroll + i
                    j = c * ny + jj
                    r, shift = row_ref[j], col_ref[j]
                    here = lane == jj
                    for q in range(groups):
                        v = scr[pl.ds(r + q * 8 * cells, 8, stride=cells), :]
                        acc[q] = jnp.where(here, pltpu.roll(v, shift, 1), acc[q])
                return tuple(acc)

            zero = jnp.zeros((8, ny), jnp.float32)
            acc = lax.fori_loop(0, ny // unroll, step, (zero,) * groups)
            for q in range(groups):
                picked_ref[q * 8 : (q + 1) * 8, pl.ds(pl.multiple_of(c * ny, ny), ny)] = acc[q]
            return carry

        lax.fori_loop(0, picked_ref.shape[1] // ny, chunk, 0)


def border(pred, u, k, ulo, klo, uhi, khi, position):
    m, cz, nx, ny = u.shape
    slots = position.shape[0]
    block = 8
    row = position // ny
    slot = jnp.arange(slots, dtype=jnp.int32)
    shift = (slot - position % ny) % ny
    edge = pl.BlockSpec((block, 1, nx, ny), lambda g, e, *_: (g, e * (cz - 1), 0, 0))
    halo = pl.BlockSpec((block, nx, ny), lambda g, e, *_: (g, 0, 0))
    return pl.pallas_call(
        border_kernel,
        grid_spec=pltpu.PrefetchScalarGridSpec(
            num_scalar_prefetch=2,
            grid=(m // block, 2),
            in_specs=[
                pl.BlockSpec((block, cz, nx, ny), lambda g, e, *_: (g, 0, 0, 0)),
                edge, edge, halo, halo, halo, halo,
            ],
            out_specs=[edge, pl.BlockSpec((m, slots), lambda g, e, *_: (0, 0))],
            scratch_shapes=[pltpu.VMEM((m * cz * nx, ny), jnp.float32)],
        ),
        out_shape=[
            jax.ShapeDtypeStruct(u.shape, jnp.float32),
            jax.ShapeDtypeStruct((m, slots), jnp.float32),
        ],
        input_output_aliases={2: 0},
        name="border",
    )(row, shift, pred, u, k, ulo, klo, uhi, khi)


def products_kernel(
    n_e, n_s, count_ref, picked_ref, noise_ref, values_ref, std_ref, params_ref,
    gram_ref, cross_ref, all_params_ref,
    all_picked, part, parts, total,
    send_a, recv_a, send_p, recv_p, send_s, recv_s, send_g, recv_g,
):
    own, slots = picked_ref.shape
    members = own * n_e
    me_e, me_s = lax.axis_index("ens"), lax.axis_index("space")
    scale = math.sqrt(members - 1.0)

    def ens_peer(d):
        return (lax.rem(me_e + d, n_e), me_s)

    def space_peer(d):
        return (me_e, lax.rem(me_s + d, n_s))

    barrier = pltpu.get_barrier_semaphore()
    for d in range(1, n_e):
        pl.semaphore_signal(barrier, inc=1, device_id=ens_peer(d), device_id_type=MESH)
    for d in range(1, n_s):
        pl.semaphore_signal(barrier, inc=1, device_id=space_peer(d), device_id_type=MESH)
    pl.semaphore_wait(barrier, n_e + n_s - 2)

    def send(src, dst, ssem, rsem, peer):
        copy = pltpu.make_async_remote_copy(
            src_ref=src, dst_ref=dst, send_sem=ssem, recv_sem=rsem,
            device_id=peer, device_id_type=MESH,
        )
        copy.start()
        return copy

    picked_copies = [
        send(picked_ref, all_picked.at[me_e], send_a.at[d], recv_a.at[d], ens_peer(d))
        for d in range(1, n_e)
    ]
    params_copies = [
        send(params_ref, all_params_ref.at[me_e], send_p.at[d], recv_p.at[d], ens_peer(d))
        for d in range(1, n_e)
    ]
    all_params_ref[me_e] = params_ref[...]
    mine = picked_ref[...]
    all_picked[me_e] = mine
    live = lax.broadcasted_iota(jnp.int32, (1, slots), 1) < count_ref[0]
    std = std_ref[...]
    inverse = jnp.where(live, 1.0 / (std * scale), 0.0)
    misfit = jnp.where(live, (values_ref[...] - mine) / std + noise_ref[...], 0.0)
    for copy in picked_copies:
        copy.wait()
    everyone = all_picked[...].reshape(members, slots)
    centre = jnp.sum(everyone, axis=0, keepdims=True) / members
    spread = (everyone - centre) * inverse
    left = jnp.concatenate([(mine - centre) * inverse, misfit], axis=0)
    part[...] = lax.dot_general(
        left, spread, (((1,), (1,)), ((), ())),
        precision=HI, preferred_element_type=jnp.float32,
    )
    space_copies = [
        send(part, parts.at[d], send_s.at[d], recv_s.at[d], space_peer(d)) for d in range(1, n_s)
    ]
    acc = part[...]
    for d in range(1, n_s):
        space_copies[d - 1].wait()
        acc += parts[d]
    total[...] = acc[:own]
    gram_copies = [
        send(total, gram_ref.at[me_e], send_g.at[d], recv_g.at[d], ens_peer(d))
        for d in range(1, n_e)
    ]
    gram_ref[me_e] = acc[:own]
    cross_ref[...] = acc[own:]
    for copy in gram_copies:
        copy.wait()
    for copy in params_copies:
        copy.wait()


def products(n_e, n_s, count, picked, noise, values, std, params):
    own, slots = picked.shape
    vmem = pl.BlockSpec(memory_space=pltpu.VMEM)
    dma = pltpu.SemaphoreType.DMA
    return pl.pallas_call(
        functools.partial(products_kernel, n_e, n_s),
        in_specs=[pl.BlockSpec(memory_space=pltpu.SMEM)] + [vmem] * 5,
        out_specs=[vmem] * 3,
        out_shape=[
            jax.ShapeDtypeStruct((n_e, own, n_e * own), jnp.float32),
            jax.ShapeDtypeStruct((own, n_e * own), jnp.float32),
            jax.ShapeDtypeStruct((n_e,) + params.shape, jnp.float32),
        ],
        scratch_shapes=[
            pltpu.VMEM((n_e, own, slots), jnp.float32),
            pltpu.VMEM((2 * own, n_e * own), jnp.float32),
            pltpu.VMEM((n_s, 2 * own, n_e * own), jnp.float32),
            pltpu.VMEM((own, n_e * own), jnp.float32),
        ]
        + [dma((n_e,))] * 4 + [dma((n_s,))] * 2 + [dma((n_e,))] * 2,
        compiler_params=pltpu.CompilerParams(collective_id=0, has_side_effects=True),
        name="products",
    )(count, picked, noise, values.reshape(1, -1), std.reshape(1, -1), params)


def update_kernel(gram_ref, cross_ref, all_params_ref, params_ref, o_ref, work):
    members = gram_ref.shape[1]
    own = cross_ref.shape[0]
    rows = lax.broadcasted_iota(jnp.int32, (members, members), 0)
    cols = lax.broadcasted_iota(jnp.int32, (members, members), 1)
    lane = lax.broadcasted_iota(jnp.int32, (1, members), 1)
    work[:members] = gram_ref[...] + jnp.where(rows == cols, 1.0, 0.0)
    work[members:] = cross_ref[...]

    def step(k, diagonal):
        here = lane == k
        row = work[pl.ds(k, 1), :]
        pivot = jnp.sum(jnp.where(here, row, 0.0), axis=1, keepdims=True)
        factor = jnp.where(here, 0.0, row / pivot)
        t = work[...]
        column = jnp.sum(jnp.where(here, t, 0.0), axis=1, keepdims=True)
        work[...] = t - column * factor
        return jnp.where(here, pivot, diagonal)

    diagonal = lax.fori_loop(0, members, step, jnp.ones((1, members), jnp.float32))
    weights = work[members:] / diagonal
    all_params = all_params_ref[...]
    centre = jnp.sum(all_params, axis=0, keepdims=True) / members
    anomaly = (all_params - centre) / math.sqrt(members - 1.0)
    o_ref[...] = params_ref[...] + jnp.dot(
        weights, anomaly, precision=HI, preferred_element_type=jnp.float32
    )


def update(gram, cross, all_params, params):
    members, own = gram.shape[2], cross.shape[0]
    return pl.pallas_call(
        update_kernel,
        out_shape=jax.ShapeDtypeStruct(params.shape, jnp.float32),
        scratch_shapes=[pltpu.VMEM((members + own, members), jnp.float32)],
        name="update",
    )(gram.reshape(members, members), cross, all_params.reshape(members, -1), params)


def shards(n_e, n_s, u, k, position, count, values, std, noise, params):
    up = [(i, i + 1) for i in range(n_s - 1)]
    down = [(i + 1, i) for i in range(n_s - 1)]
    ulo = lax.ppermute(u[:, -1], "space", up)
    klo = lax.ppermute(k[:, -1], "space", up)
    uhi = lax.ppermute(u[:, 0], "space", down)
    khi = lax.ppermute(k[:, 0], "space", down)
    pred = stencil(u, k)
    pred, picked = border(pred, u, k, ulo, klo, uhi, khi, position)
    gram, cross, all_params = products(n_e, n_s, count, picked, noise, values, std, params)
    return update(gram, cross, all_params, params), pred


def solution(mesh):
    in_specs = (
        P("ens", "space", None, None),
        P("ens", "space", None, None),
        P("space"),
        P("space"),
        P("space"),
        P("space"),
        P("ens", "space"),
        P("ens", "space"),
    )
    out_specs = (P("ens", "space"), P("ens", "space", None, None))
    body = functools.partial(shards, mesh.shape["ens"], mesh.shape["space"])
    return jax.shard_map(body, mesh=mesh, in_specs=in_specs, out_specs=out_specs, check_vma=False)
```

time: 346 us -> 130 us (0.38)
  other arithmetic: 132 us -> 0.61 us
  Pallas kernels: 0 us -> 89.9 us
  waiting for transfers between devices: 103 us -> 21 us
  local copies, waits for them, and re-layouts: 64.6 us -> 5.3 us
  blocking collectives: 20.1 us -> 0 us
  between operations: 14.9 us -> 1.35 us
  matrix products: 4.87 us -> 0 us
  starting transfers between devices: 6.25 us -> 10.9 us
    pallas_call x0 -> x4, Pallas kernels: none -> 89.9 us  [the longest x1 36.3 us: border(): pl.pallas_call(border_kernel, grid_spec=pltpu.PrefetchScalarGridSpec(num_...]
    add x2 -> x0, other arithmetic: 80.1 us -> none  [the longest x1 79.3 us: spread_heat_onestep(): return centre_u + step_size * flux]
    psum x1 -> x0, waiting for transfers between devices: 72.7 us -> none  [shards(): gram_matrix, cross_part = lax.psum((gram_matrix, cross_part), 'space')]
    squeeze x1 -> x2, local copies, waits for them, and re-layouts: 31.1 us -> 4.15 us  [the longest x1 2.08 us: shards(): uhi = lax.ppermute(u[:, 0], 'space', down)]
    pad x1 -> x0, other arithmetic: 24.4 us -> none  [shards(): jnp.pad(bordered_profile.astype(jnp.float32), ((0, 0), (0, 0), (0, 0), (1...]
    another operation x5 -> x0, other arithmetic: 22.9 us -> none  [the longest x3 12.4 us: shards(): jnp.linalg.cholesky(gram_matrix + jnp.eye(ensemble, dtype=jnp.float32))]
    all_gather x3 -> x0, blocking collectives: 20.1 us -> none  [the longest x1 7.37 us: shards(): lax.all_gather(sampled_readings, 'ens', axis=0, tiled=True)]
    add x2 -> x0, local copies, waits for them, and re-layouts: 19.9 us -> none  [the longest x1 19.8 us: spread_heat_onestep(): return centre_u + step_size * flux]
  transfers between devices with their start and end apart: 3 -> 4, of which waited for: 2 -> 2; matrix products, arithmetic and copies ran while one was open for 0% -> 2% of each run, Pallas kernels for 0% -> 11%
where the time goes in v1:
time: 130 us; the launch traced here: 129 us
  Pallas kernels  89.9 us (69%)
  waiting for transfers between devices  21 us (16%)
  starting transfers between devices  10.9 us (8%)
  local copies, waits for them, and re-layouts  5.3 us (4%)
  between operations  1.35 us (1%)
    pallas_call x1, Pallas kernels, border(): pl.pallas_call(border_kernel, grid_spec=pltpu.PrefetchScalarGridSpec(num_...  36.3 us
    pallas_call x1, Pallas kernels, products(): pl.pallas_call(functools.partial(products_kernel, n_e, n_s), in_specs=[pl...  24 us
    pallas_call x1, Pallas kernels, update(): pl.pallas_call(update_kernel, out_shape=jax.ShapeDtypeStruct(params.shape...  14.9 us
    pallas_call x1, Pallas kernels, stencil(): pl.pallas_call(stencil_kernel, grid=(m // block,), in_specs=[spec, spec],...  14.7 us
    ppermute x1, waiting for transfers between devices, shards(): ulo = lax.ppermute(u[:, -1], 'space', up)  10.9 us
    ppermute x1, waiting for transfers between devices, shards(): klo = lax.ppermute(k[:, -1], 'space', up)  10.1 us
    ppermute x1, starting transfers between devices, shards(): ulo = lax.ppermute(u[:, -1], 'space', up)  4.89 us
    ppermute x1, starting transfers between devices, shards(): klo = lax.ppermute(k[:, -1], 'space', up)  3.44 us
  transfers between devices with their start and end apart: 4, of which 2 were waited for; matrix products, arithmetic and copies ran while one was open for 2% of the time, Pallas kernels for 11%

profile of v1, /device:TPU:0, one launch (start us, length us, event | category | flops | bytes accessed | tf_op | source)
XLA Modules:
  0.0 129.1 jit_solution(17204093865539053966)
XLA Ops:
  0.6 2.1 %slice_bitcast_fusion.1 = (bf16[32,64,128]{2,1,0:T(8,128)(2,1)S(1)}, bf16[32,64,128]{2,1,0:T(8,128)(2,1)}) fusion(bf16[32,8,64,128]{3,2,1,0:T(8,128)(2,1)} %u_ref.3), kind=kLoop, calls=%fused_computation.1 | loop fusion | bytes 2097152 | tf_op jit(solution)/shard_map/squeeze | solution.py:302
  2.7 4.9 %collective-permute-start = (bf16[32,64,128]{2,1,0:T(8,128)(2,1)}, bf16[32,64,128]{2,1,0:T(8,128)(2,1)S(1)}, u32[]{:S(2)}, u32[]{:S(2)}) collective-permute-start(bf16[32,64,128]{2,1,0:T(8,128)(2,1)} %get-tuple-element.15), channel_id=1, source_target_pairs={{0,1},{1,2},{2,3},{3,4},{4,5},{5,6},{6,7},{8,9},{9,10},{10,11},{11... | collective-permute-start | bytes 1572872 | tf_op jit(solution)/shard_map/ppermute | solution.py:300
  7.6 2.1 %slice_bitcast_fusion = (bf16[32,64,128]{2,1,0:T(8,128)(2,1)S(1)}, bf16[32,64,128]{2,1,0:T(8,128)(2,1)}) fusion(bf16[32,8,64,128]{3,2,1,0:T(8,128)(2,1)} %k_ref.3), kind=kLoop, calls=%fused_computation | loop fusion | bytes 2097152 | tf_op jit(solution)/shard_map/squeeze | solution.py:303
  9.7 3.4 %collective-permute-start.1 = (bf16[32,64,128]{2,1,0:T(8,128)(2,1)}, bf16[32,64,128]{2,1,0:T(8,128)(2,1)S(1)}, u32[]{:S(2)}, u32[]{:S(2)}) collective-permute-start(bf16[32,64,128]{2,1,0:T(8,128)(2,1)} %get-tuple-element.13), channel_id=1, source_target_pairs={{0,1},{1,2},{2,3},{3,4},{4,5},{5,6},{6,7},{8,9},{9,10},{10,11},{11... | collective-permute-start | bytes 1572872 | tf_op jit(solution)/shard_map/ppermute | solution.py:301
  13.1 1.3 %collective-permute-start.2 = (bf16[32,64,128]{2,1,0:T(8,128)(2,1)S(1)}, bf16[32,64,128]{2,1,0:T(8,128)(2,1)S(1)}, u32[]{:S(2)}, u32[]{:S(2)}) collective-permute-start(bf16[32,64,128]{2,1,0:T(8,128)(2,1)S(1)} %get-tuple-element.14), channel_id=1, source_target_pairs={{1,0},{2,1},{3,2},{4,3},{5,4},{6,5},{7,6},{9,8},{10,9},{11,10},{12... | collective-permute-start | bytes 1572872 | tf_op jit(solution)/shard_map/ppermute | solution.py:302
  14.4 1.3 %collective-permute-start.3 = (bf16[32,64,128]{2,1,0:T(8,128)(2,1)S(1)}, bf16[32,64,128]{2,1,0:T(8,128)(2,1)S(1)}, u32[]{:S(2)}, u32[]{:S(2)}) collective-permute-start(bf16[32,64,128]{2,1,0:T(8,128)(2,1)S(1)} %get-tuple-element.12), channel_id=1, source_target_pairs={{1,0},{2,1},{3,2},{4,3},{5,4},{6,5},{7,6},{9,8},{10,9},{11,10},{12... | collective-permute-start | bytes 1572872 | tf_op jit(solution)/shard_map/ppermute | solution.py:303
  16.4 0.0 copy-start.4
  16.4 14.7 %stencil.1.p_ref = f32[32,8,64,128]{3,2,1,0:T(8,128)} custom-call(bf16[32,8,64,128]{3,2,1,0:T(8,128)(2,1)} %u_ref.3, bf16[32,8,64,128]{3,2,1,0:T(8,128)(2,1)} %k_ref.3), custom_call_target="tpu_custom_call" | custom-call | flops 83886080 | bytes 16777216 | tf_op jit(solution)/shard_map/stencil/pallas_call | solution.py:52
  31.1 0.0 copy-done.4
  31.1 0.6 add_select_fusion
  31.7 10.9 %collective-permute-done.ulo_ref = bf16[32,64,128]{2,1,0:T(8,128)(2,1)S(1)} collective-permute-done((bf16[32,64,128]{2,1,0:T(8,128)(2,1)}, bf16[32,64,128]{2,1,0:T(8,128)(2,1)S(1)}, u32[]{:S(2)}, u32[]{:S(2)}) %collective-permute-start) | collective-permute-done | bytes 524320 | tf_op jit(solution)/shard_map/ppermute | solution.py:300
  42.7 0.0 copy-start
  42.7 10.1 %collective-permute-done.1.klo_ref = bf16[32,64,128]{2,1,0:T(8,128)(2,1)S(1)} collective-permute-done((bf16[32,64,128]{2,1,0:T(8,128)(2,1)}, bf16[32,64,128]{2,1,0:T(8,128)(2,1)S(1)}, u32[]{:S(2)}, u32[]{:S(2)}) %collective-permute-start.1) | collective-permute-done | bytes 524320 | tf_op jit(solution)/shard_map/ppermute | solution.py:301
  52.8 0.0 copy-start.1
  52.8 0.0 collective-permute-done.2.uhi_ref
  52.8 0.0 copy-start.2
  52.8 0.0 collective-permute-done.3.khi_ref
  52.8 0.0 copy-start.3
  52.8 0.0 copy-done
  52.8 0.8 copy-done.1
  53.5 0.2 copy-done.2
  53.8 0.2 copy-done.3
  53.9 36.3 %border.1 = (f32[32,8,64,128]{3,2,1,0:T(8,128)}, f32[32,1024]{1,0:T(8,128)}) custom-call(s32[1024]{0:T(1024)} %get-tuple-element.17.row_ref, s32[1024]{0:T(1024)} %get-tuple-element.16.col_ref, f32[32,8,64,128]{3,2,1,0:T(8,128)} %stencil.1.p_ref, bf16[32,8,64,128]{3,2,1,0:T(8,128)(2,1)} %u_ref.3, ...), custom_call_target="tpu_custom_call", output_to_operand_aliasing={{0}: (2, {})} | custom-call | tf_op jit(solution)/shard_map/border/pallas_call | solution.py:135
  90.2 24.0 %products.1 = (f32[4,32,128]{2,1,0:T(8,128)}, f32[32,128]{1,0:T(8,128)}, f32[4,32,256]{2,1,0:T(8,128)}) custom-call(s32[1]{0:T(128)S(6)} %copy.20.count_ref, f32[32,1024]{1,0:T(8,128)} %get-tuple-element.7.picked_ref, f32[32,1024]{1,0:T(8,128)} %noise_ref.1, f32[1,1024]{1,0:T(1,128)} %bitcast.22, f32[1,1024]{1,0:T(1,128)} %bitcast.23, f32[32,256]{1,0:T(8,128)} %params_ref.3), custom_call_target="tpu_custom_call" | custom-call | tf_op jit(solution)/shard_map/products/pallas_call | solution.py:237
  114.2 14.9 %update.1 = f32[32,256]{1,0:T(8,128)} custom-call(f32[128,128]{1,0:T(8,128)} %bitcast.21, f32[32,128]{1,0:T(8,128)} %get-tuple-element.9.cross_ref, f32[128,256]{1,0:T(8,128)} %bitcast.20, f32[32,256]{1,0:T(8,128)} %params_ref.3), custom_call_target="tpu_custom_call" | custom-call | tf_op jit(solution)/shard_map/update/pallas_call | solution.py:289
Async XLA Ops:
  2.7 39.9 %collective-permute-start = (bf16[32,64,128]{2,1,0:T(8,128)(2,1)}, bf16[32,64,128]{2,1,0:T(8,128)(2,1)S(1)}, u32[]{:S(2)}, u32[]{:S(2)}) collective-permute-start(bf16[32,64,128]{2,1,0:T(8,128)(2,1)} %get-tuple-element.15), channel_id=1, source_target_pairs={{0,1},{1,2},{2,3},{3,4},{4,5},{5,6},{6,7},{8,9},{9,10},{10,11},{11... | collective-permute-start | bytes 1572872 | tf_op jit(solution)/shard_map/ppermute | solution.py:300
  9.7 43.1 %collective-permute-start.1 = (bf16[32,64,128]{2,1,0:T(8,128)(2,1)}, bf16[32,64,128]{2,1,0:T(8,128)(2,1)S(1)}, u32[]{:S(2)}, u32[]{:S(2)}) collective-permute-start(bf16[32,64,128]{2,1,0:T(8,128)(2,1)} %get-tuple-element.13), channel_id=1, source_target_pairs={{0,1},{1,2},{2,3},{3,4},{4,5},{5,6},{6,7},{8,9},{9,10},{10,11},{11... | collective-permute-start | bytes 1572872 | tf_op jit(solution)/shard_map/ppermute | solution.py:301
  13.1 39.6 %collective-permute-start.2 = (bf16[32,64,128]{2,1,0:T(8,128)(2,1)S(1)}, bf16[32,64,128]{2,1,0:T(8,128)(2,1)S(1)}, u32[]{:S(2)}, u32[]{:S(2)}) collective-permute-start(bf16[32,64,128]{2,1,0:T(8,128)(2,1)S(1)} %get-tuple-element.14), channel_id=1, source_target_pairs={{1,0},{2,1},{3,2},{4,3},{5,4},{6,5},{7,6},{9,8},{10,9},{11,10},{12... | collective-permute-start | bytes 1572872 | tf_op jit(solution)/shard_map/ppermute | solution.py:302
  14.4 38.3 %collective-permute-start.3 = (bf16[32,64,128]{2,1,0:T(8,128)(2,1)S(1)}, bf16[32,64,128]{2,1,0:T(8,128)(2,1)S(1)}, u32[]{:S(2)}, u32[]{:S(2)}) collective-permute-start(bf16[32,64,128]{2,1,0:T(8,128)(2,1)S(1)} %get-tuple-element.12), channel_id=1, source_target_pairs={{1,0},{2,1},{3,2},{4,3},{5,4},{6,5},{7,6},{9,8},{10,9},{11,10},{12... | collective-permute-start | bytes 1572872 | tf_op jit(solution)/shard_map/ppermute | solution.py:303
  16.4 14.7 %copy-start.4 = (s32[1024]{0:T(1024)S(1)}, s32[1024]{0:T(1024)}, u32[]{:S(2)}) copy-start(s32[1024]{0:T(1024)} %param.10) | copy-start | bytes 12292
  42.7 10.1 %copy-start = (bf16[32,64,128]{2,1,0:T(8,128)(2,1)}, bf16[32,64,128]{2,1,0:T(8,128)(2,1)S(1)}, u32[]{:S(2)}) copy-start(bf16[32,64,128]{2,1,0:T(8,128)(2,1)S(1)} %collective-permute-done.ulo_ref) | copy-start | bytes 1572868
  52.8 0.8 copy-start.1
  52.8 1.0 copy-start.2
  52.8 1.2 copy-start.3

commit v2 on v1

--- a/solution.py
+++ b/solution.py
@@ -13,7 +13,7 @@
 MESH = pl.DeviceIdType.MESH
 
 
-def stencil_kernel(u_ref, k_ref, o_ref):
+def stencil_kernel(u_ref, k_ref, o_ref, t_ref):
     members, cz, nx, ny = u_ref.shape
     row = lax.broadcasted_iota(jnp.int32, (nx, ny), 0)
     lane = lax.broadcasted_iota(jnp.int32, (nx, ny), 1)
@@ -44,17 +44,28 @@
 
     lax.fori_loop(0, members, member, 0)
 
+    def turn(z, carry):
+        for x in range(0, nx, 8):
+            tile = o_ref[:, z, x : x + 8, :]
+            t_ref[pl.ds(pl.multiple_of(z * nx, nx) + x, 8)] = jnp.swapaxes(tile, 0, 1)
+        return carry
+
+    lax.fori_loop(0, cz, turn, 0)
+
 
 def stencil(u, k):
     m, cz, nx, ny = u.shape
-    block = 4
+    block = 8
     spec = pl.BlockSpec((block, cz, nx, ny), lambda g: (g, 0, 0, 0))
     return pl.pallas_call(
         stencil_kernel,
         grid=(m // block,),
         in_specs=[spec, spec],
-        out_specs=spec,
-        out_shape=jax.ShapeDtypeStruct(u.shape, jnp.float32),
+        out_specs=[spec, pl.BlockSpec((cz * nx, block, ny), lambda g: (0, g, 0))],
+        out_shape=[
+            jax.ShapeDtypeStruct(u.shape, jnp.float32),
+            jax.ShapeDtypeStruct((cz * nx, m, ny), jnp.float32),
+        ],
         cost_estimate=pl.CostEstimate(
             flops=40 * u.size, bytes_accessed=8 * u.size, transcendentals=0
         ),
@@ -63,67 +74,62 @@
 
 
 def border_kernel(
-    row_ref, col_ref, p_ref, u_ref, k_ref, ulo_ref, klo_ref, uhi_ref, khi_ref,
-    o_ref, picked_ref, scr,
+    row_ref, col_ref, p_ref, u_ref, k_ref, ulo_ref, klo_ref, uhi_ref, khi_ref, turned_ref,
+    o_ref, picked_ref, scr, sem,
 ):
     g, e = pl.program_id(0), pl.program_id(1)
-    block, cz, nx, ny = p_ref.shape
-    cells = cz * nx
-    members = scr.shape[0] // cells
-    base = g * block
+    block, _, nx, ny = p_ref.shape
+    cells, members, _ = scr.shape
+    inner = pl.ds(nx, cells - 2 * nx)
+    load = pltpu.make_async_copy(turned_ref.at[inner], scr.at[inner], sem)
     u = u_ref[:, 0].astype(jnp.float32)
     k = k_ref[:, 0].astype(jnp.float32)
-
-    def fix(z, un_ref, kn_ref):
+    own = pl.ds(pl.multiple_of(g * block, block), block)
+
+    def fix(row, un_ref, kn_ref):
         un = un_ref[...].astype(jnp.float32)
         kn = kn_ref[...].astype(jnp.float32)
-        new = p_ref[:, z] + half_step * (k + kn) * (un - u)
+        new = p_ref[:, 0] + half_step * (k + kn) * (un - u)
         o_ref[:, 0] = new
-        for b in range(block):
-            start = pl.multiple_of((base + b) * cells + z * nx, nx)
-            scr[pl.ds(start, nx), :] = new[b]
+        for x in range(0, nx, 8):
+            scr[row + x : row + x + 8, own, :] = jnp.swapaxes(new[:, x : x + 8, :], 0, 1)
+
+    @pl.when(jnp.logical_and(g == 0, e == 0))
+    def _():
+        load.start()
 
     @pl.when(e == 0)
     def _():
         fix(0, ulo_ref, klo_ref)
-        for b in range(block):
-            for z in range(1, cz - 1):
-                start = pl.multiple_of((base + b) * cells + z * nx, nx)
-                scr[pl.ds(start, nx), :] = p_ref[b, z]
 
     @pl.when(e == 1)
     def _():
-        fix(cz - 1, uhi_ref, khi_ref)
+        fix(cells - nx, uhi_ref, khi_ref)
 
     @pl.when(jnp.logical_and(g == pl.num_programs(0) - 1, e == 1))
     def _():
-        lane = lax.broadcasted_iota(jnp.int32, (8, ny), 1)
-        groups = members // 8
+        load.wait()
+        lane = lax.broadcasted_iota(jnp.int32, (members, ny), 1)
         unroll = 8
 
         def chunk(c, carry):
             def step(s, acc):
-                acc = list(acc)
                 for i in range(unroll):
                     jj = s * unroll + i
                     j = c * ny + jj
-                    r, shift = row_ref[j], col_ref[j]
-                    here = lane == jj
-                    for q in range(groups):
-                        v = scr[pl.ds(r + q * 8 * cells, 8, stride=cells), :]
-                        acc[q] = jnp.where(here, pltpu.roll(v, shift, 1), acc[q])
-                return tuple(acc)
-
-            zero = jnp.zeros((8, ny), jnp.float32)
-            acc = lax.fori_loop(0, ny // unroll, step, (zero,) * groups)
-            for q in range(groups):
-                picked_ref[q * 8 : (q + 1) * 8, pl.ds(pl.multiple_of(c * ny, ny), ny)] = acc[q]
+                    v = pltpu.roll(scr[row_ref[j]], col_ref[j], 1)
+                    acc = jnp.where(lane == jj, v, acc)
+                return acc
+
+            zero = jnp.zeros((members, ny), jnp.float32)
+            acc = lax.fori_loop(0, ny // unroll, step, zero)
+            picked_ref[:, pl.ds(pl.multiple_of(c * ny, ny), ny)] = acc
             return carry
 
         lax.fori_loop(0, picked_ref.shape[1] // ny, chunk, 0)
 
 
-def border(pred, u, k, ulo, klo, uhi, khi, position):
+def border(pred, turned, u, k, ulo, klo, uhi, khi, position):
     m, cz, nx, ny = u.shape
     slots = position.shape[0]
     block = 8
@@ -137,12 +143,10 @@
         grid_spec=pltpu.PrefetchScalarGridSpec(
             num_scalar_prefetch=2,
             grid=(m // block, 2),
-            in_specs=[
-                pl.BlockSpec((block, cz, nx, ny), lambda g, e, *_: (g, 0, 0, 0)),
-                edge, edge, halo, halo, halo, halo,
-            ],
+            in_specs=[edge, edge, edge, halo, halo, halo, halo]
+            + [pl.BlockSpec(memory_space=pl.ANY)],
             out_specs=[edge, pl.BlockSpec((m, slots), lambda g, e, *_: (0, 0))],
-            scratch_shapes=[pltpu.VMEM((m * cz * nx, ny), jnp.float32)],
+            scratch_shapes=[pltpu.VMEM(turned.shape, jnp.float32), pltpu.SemaphoreType.DMA],
         ),
         out_shape=[
             jax.ShapeDtypeStruct(u.shape, jnp.float32),
@@ -150,7 +154,7 @@
         ],
         input_output_aliases={2: 0},
         name="border",
-    )(row, shift, pred, u, k, ulo, klo, uhi, khi)
+    )(row, shift, pred, u, k, ulo, klo, uhi, khi, turned)
 
 
 def products_kernel(
@@ -264,17 +268,37 @@
     work[:members] = gram_ref[...] + jnp.where(rows == cols, 1.0, 0.0)
     work[members:] = cross_ref[...]
 
-    def step(k, diagonal):
-        here = lane == k
-        row = work[pl.ds(k, 1), :]
-        pivot = jnp.sum(jnp.where(here, row, 0.0), axis=1, keepdims=True)
-        factor = jnp.where(here, 0.0, row / pivot)
+    pivots = 4
+
+    def step(s, diagonal):
+        first = s * pivots
         t = work[...]
-        column = jnp.sum(jnp.where(here, t, 0.0), axis=1, keepdims=True)
-        work[...] = t - column * factor
-        return jnp.where(here, pivot, diagonal)
-
-    diagonal = lax.fori_loop(0, members, step, jnp.ones((1, members), jnp.float32))
+        here = [lane == first + i for i in range(pivots)]
+        columns = [
+            jnp.sum(jnp.where(here[i], t, 0.0), axis=1, keepdims=True) for i in range(pivots)
+        ]
+        rows = [work[pl.ds(first + i, 1), :] for i in range(pivots)]
+        corner = [
+            [jnp.sum(jnp.where(here[j], rows[i], 0.0), axis=1, keepdims=True) for j in range(pivots)]
+            for i in range(pivots)
+        ]
+        for i in range(pivots):
+            pivot = corner[i][i]
+            diagonal = jnp.where(here[i], pivot, diagonal)
+            inverse = 1.0 / pivot
+            factor = jnp.where(here[i], 0.0, rows[i] * inverse)
+            t = t - columns[i] * factor
+            for j in range(i + 1, pivots):
+                ratio = corner[i][j] * inverse
+                columns[j] = columns[j] - columns[i] * ratio
+                rows[j] = rows[j] - corner[j][i] * factor
+                for l in range(i + 1, pivots):
+                    corner[l][j] = corner[l][j] - corner[l][i] * ratio
+        work[...] = t
+        return diagonal
+
+    ones = jnp.ones((1, members), jnp.float32)
+    diagonal = lax.fori_loop(0, members // pivots, step, ones)
     weights = work[members:] / diagonal
     all_params = all_params_ref[...]
     centre = jnp.sum(all_params, axis=0, keepdims=True) / members
@@ -301,8 +325,8 @@
     klo = lax.ppermute(k[:, -1], "space", up)
     uhi = lax.ppermute(u[:, 0], "space", down)
     khi = lax.ppermute(k[:, 0], "space", down)
-    pred = stencil(u, k)
-    pred, picked = border(pred, u, k, ulo, klo, uhi, khi, position)
+    pred, turned = stencil(u, k)
+    pred, picked = border(pred, turned, u, k, ulo, klo, uhi, khi, position)
     gram, cross, all_params = products(n_e, n_s, count, picked, noise, values, std, params)
     return update(gram, cross, all_params, params), pred
 

time: 130 us -> 109 us (0.84)
  Pallas kernels: 89.9 us -> 72.4 us
  waiting for transfers between devices: 21 us -> 17.9 us
    pallas_call x1, Pallas kernels: 36.3 us -> 22.8 us  [border(): pl.pallas_call(border_kernel, grid_spec=pltpu.PrefetchScalarGridSpec(num_...]
    pallas_call x1, Pallas kernels: 14.9 us -> 7.68 us  [update(): pl.pallas_call(update_kernel, out_shape=jax.ShapeDtypeStruct(params.shape...]
    ppermute x1, waiting for transfers between devices: 10.9 us -> 7.74 us  [shards(): ulo = lax.ppermute(u[:, -1], 'space', up)]
    pallas_call x1, Pallas kernels: 14.7 us -> 17.9 us  [stencil(): pl.pallas_call(stencil_kernel, grid=(m // block,), in_specs=[spec, spec],...]
  transfers between devices with their start and end apart: 4 -> 4, of which waited for: 2 -> 2; matrix products, arithmetic and copies ran while one was open for 2% -> 3% of each run, Pallas kernels for 11% -> 16%
where the time goes in v2:
time: 109 us; the launch traced here: 108 us
  Pallas kernels  72.4 us (66%)
  waiting for transfers between devices  17.9 us (16%)
  starting transfers between devices  10.9 us (10%)
  local copies, waits for them, and re-layouts  5.36 us (5%)
  between operations  1.36 us (1%)
    pallas_call x1, Pallas kernels, products(): pl.pallas_call(functools.partial(products_kernel, n_e, n_s), in_specs=[pl...  24 us
    pallas_call x1, Pallas kernels, border(): pl.pallas_call(border_kernel, grid_spec=pltpu.PrefetchScalarGridSpec(num_...  22.8 us
    pallas_call x1, Pallas kernels, stencil(): pl.pallas_call(stencil_kernel, grid=(m // block,), in_specs=[spec, spec],...  17.9 us
    ppermute x1, waiting for transfers between devices, shards(): klo = lax.ppermute(k[:, -1], 'space', up)  10.1 us
    ppermute x1, waiting for transfers between devices, shards(): ulo = lax.ppermute(u[:, -1], 'space', up)  7.74 us
    pallas_call x1, Pallas kernels, update(): pl.pallas_call(update_kernel, out_shape=jax.ShapeDtypeStruct(params.shape...  7.68 us
    ppermute x1, starting transfers between devices, shards(): ulo = lax.ppermute(u[:, -1], 'space', up)  4.89 us
    ppermute x1, starting transfers between devices, shards(): klo = lax.ppermute(k[:, -1], 'space', up)  3.44 us
  transfers between devices with their start and end apart: 4, of which 2 were waited for; matrix products, arithmetic and copies ran while one was open for 3% of the time, Pallas kernels for 16%

profile of v2, /device:TPU:0, one launch (start us, length us, event | category | flops | bytes accessed | tf_op | source)
XLA Modules:
  0.0 108.5 jit_solution(13746133952412652075)
XLA Ops:
  0.6 2.1 %slice_bitcast_fusion.1 = (bf16[32,64,128]{2,1,0:T(8,128)(2,1)S(1)}, bf16[32,64,128]{2,1,0:T(8,128)(2,1)}) fusion(bf16[32,8,64,128]{3,2,1,0:T(8,128)(2,1)} %u_ref.3), kind=kLoop, calls=%fused_computation.1 | loop fusion | bytes 2097152 | tf_op jit(solution)/shard_map/squeeze | solution.py:326
  2.7 4.9 %collective-permute-start = (bf16[32,64,128]{2,1,0:T(8,128)(2,1)}, bf16[32,64,128]{2,1,0:T(8,128)(2,1)S(1)}, u32[]{:S(2)}, u32[]{:S(2)}) collective-permute-start(bf16[32,64,128]{2,1,0:T(8,128)(2,1)} %get-tuple-element.19), channel_id=1, source_target_pairs={{0,1},{1,2},{2,3},{3,4},{4,5},{5,6},{6,7},{8,9},{9,10},{10,11},{11... | collective-permute-start | bytes 1572872 | tf_op jit(solution)/shard_map/ppermute | solution.py:324
  7.6 2.1 %slice_bitcast_fusion = (bf16[32,64,128]{2,1,0:T(8,128)(2,1)S(1)}, bf16[32,64,128]{2,1,0:T(8,128)(2,1)}) fusion(bf16[32,8,64,128]{3,2,1,0:T(8,128)(2,1)} %k_ref.3), kind=kLoop, calls=%fused_computation | loop fusion | bytes 2097152 | tf_op jit(solution)/shard_map/squeeze | solution.py:327
  9.7 3.4 %collective-permute-start.1 = (bf16[32,64,128]{2,1,0:T(8,128)(2,1)}, bf16[32,64,128]{2,1,0:T(8,128)(2,1)S(1)}, u32[]{:S(2)}, u32[]{:S(2)}) collective-permute-start(bf16[32,64,128]{2,1,0:T(8,128)(2,1)} %get-tuple-element.17), channel_id=1, source_target_pairs={{0,1},{1,2},{2,3},{3,4},{4,5},{5,6},{6,7},{8,9},{9,10},{10,11},{11... | collective-permute-start | bytes 1572872 | tf_op jit(solution)/shard_map/ppermute | solution.py:325
  13.2 1.3 %collective-permute-start.2 = (bf16[32,64,128]{2,1,0:T(8,128)(2,1)S(1)}, bf16[32,64,128]{2,1,0:T(8,128)(2,1)S(1)}, u32[]{:S(2)}, u32[]{:S(2)}) collective-permute-start(bf16[32,64,128]{2,1,0:T(8,128)(2,1)S(1)} %get-tuple-element.18), channel_id=1, source_target_pairs={{1,0},{2,1},{3,2},{4,3},{5,4},{6,5},{7,6},{9,8},{10,9},{11,10},{12... | collective-permute-start | bytes 1572872 | tf_op jit(solution)/shard_map/ppermute | solution.py:326
  14.5 1.3 %collective-permute-start.3 = (bf16[32,64,128]{2,1,0:T(8,128)(2,1)S(1)}, bf16[32,64,128]{2,1,0:T(8,128)(2,1)S(1)}, u32[]{:S(2)}, u32[]{:S(2)}) collective-permute-start(bf16[32,64,128]{2,1,0:T(8,128)(2,1)S(1)} %get-tuple-element.16), channel_id=1, source_target_pairs={{1,0},{2,1},{3,2},{4,3},{5,4},{6,5},{7,6},{9,8},{10,9},{11,10},{12... | collective-permute-start | bytes 1572872 | tf_op jit(solution)/shard_map/ppermute | solution.py:327
  16.4 0.0 copy-start.4
  16.4 17.9 %stencil.1 = (f32[32,8,64,128]{3,2,1,0:T(8,128)}, f32[512,32,128]{2,1,0:T(8,128)}) custom-call(bf16[32,8,64,128]{3,2,1,0:T(8,128)(2,1)} %u_ref.3, bf16[32,8,64,128]{3,2,1,0:T(8,128)(2,1)} %k_ref.3), custom_call_target="tpu_custom_call" | custom-call | flops 83886080 | bytes 16777216 | tf_op jit(solution)/shard_map/stencil/pallas_call | solution.py:60
  34.3 0.0 copy-done.4
  34.3 0.6 add_select_fusion
  34.9 7.7 %collective-permute-done.ulo_ref = bf16[32,64,128]{2,1,0:T(8,128)(2,1)S(1)} collective-permute-done((bf16[32,64,128]{2,1,0:T(8,128)(2,1)}, bf16[32,64,128]{2,1,0:T(8,128)(2,1)S(1)}, u32[]{:S(2)}, u32[]{:S(2)}) %collective-permute-start) | collective-permute-done | bytes 524320 | tf_op jit(solution)/shard_map/ppermute | solution.py:324
  42.7 0.0 copy-start
  42.7 10.1 %collective-permute-done.1.klo_ref = bf16[32,64,128]{2,1,0:T(8,128)(2,1)S(1)} collective-permute-done((bf16[32,64,128]{2,1,0:T(8,128)(2,1)}, bf16[32,64,128]{2,1,0:T(8,128)(2,1)S(1)}, u32[]{:S(2)}, u32[]{:S(2)}) %collective-permute-start.1) | collective-permute-done | bytes 524320 | tf_op jit(solution)/shard_map/ppermute | solution.py:325
  52.8 0.0 copy-start.1
  52.8 0.0 collective-permute-done.2.uhi_ref
  52.8 0.0 copy-start.2
  52.8 0.0 collective-permute-done.3.khi_ref
  52.8 0.0 copy-start.3
  52.8 0.0 copy-done
  52.8 0.8 copy-done.1
  53.6 0.1 copy-done.2
  53.8 0.2 copy-done.3
  54.0 22.8 %border.1 = (f32[32,8,64,128]{3,2,1,0:T(8,128)}, f32[32,1024]{1,0:T(8,128)}) custom-call(s32[1024]{0:T(1024)} %get-tuple-element.21.row_ref, s32[1024]{0:T(1024)} %get-tuple-element.20.col_ref, f32[32,8,64,128]{3,2,1,0:T(8,128)} %get-tuple-element.9.p_ref, bf16[32,8,64,128]{3,2,1,0:T(8,128)(2,1)} %u_ref.3, ...), custom_call_target="tpu_custom_call", output_to_operand_aliasing={{0}: (2, {})} | custom-call | tf_op jit(solution)/shard_map/border/pallas_call | solution.py:141
  76.8 24.0 %products.1 = (f32[4,32,128]{2,1,0:T(8,128)}, f32[32,128]{1,0:T(8,128)}, f32[4,32,256]{2,1,0:T(8,128)}) custom-call(s32[1]{0:T(128)S(6)} %copy.20.count_ref, f32[32,1024]{1,0:T(8,128)} %get-tuple-element.11.picked_ref, f32[32,1024]{1,0:T(8,128)} %noise_ref.1, f32[1,1024]{1,0:T(1,128)} %bitcast.22, f32[1,1024]{1,0:T(1,128)} %bitcast.23, f32[32,256]{1,0:T(8,128)} %params_ref.3), custom_call_target="tpu_custom_call" | custom-call | tf_op jit(solution)/shard_map/products/pallas_call | solution.py:241
  100.8 7.7 %update.1 = f32[32,256]{1,0:T(8,128)} custom-call(f32[128,128]{1,0:T(8,128)} %bitcast.21, f32[32,128]{1,0:T(8,128)} %get-tuple-element.13.cross_ref, f32[128,256]{1,0:T(8,128)} %bitcast.20, f32[32,256]{1,0:T(8,128)} %params_ref.3), custom_call_target="tpu_custom_call" | custom-call | tf_op jit(solution)/shard_map/update/pallas_call | solution.py:313
Async XLA Ops:
  2.7 39.9 %collective-permute-start = (bf16[32,64,128]{2,1,0:T(8,128)(2,1)}, bf16[32,64,128]{2,1,0:T(8,128)(2,1)S(1)}, u32[]{:S(2)}, u32[]{:S(2)}) collective-permute-start(bf16[32,64,128]{2,1,0:T(8,128)(2,1)} %get-tuple-element.19), channel_id=1, source_target_pairs={{0,1},{1,2},{2,3},{3,4},{4,5},{5,6},{6,7},{8,9},{9,10},{10,11},{11... | collective-permute-start | bytes 1572872 | tf_op jit(solution)/shard_map/ppermute | solution.py:324
  9.7 43.0 %collective-permute-start.1 = (bf16[32,64,128]{2,1,0:T(8,128)(2,1)}, bf16[32,64,128]{2,1,0:T(8,128)(2,1)S(1)}, u32[]{:S(2)}, u32[]{:S(2)}) collective-permute-start(bf16[32,64,128]{2,1,0:T(8,128)(2,1)} %get-tuple-element.17), channel_id=1, source_target_pairs={{0,1},{1,2},{2,3},{3,4},{4,5},{5,6},{6,7},{8,9},{9,10},{10,11},{11... | collective-permute-start | bytes 1572872 | tf_op jit(solution)/shard_map/ppermute | solution.py:325
  13.2 39.6 %collective-permute-start.2 = (bf16[32,64,128]{2,1,0:T(8,128)(2,1)S(1)}, bf16[32,64,128]{2,1,0:T(8,128)(2,1)S(1)}, u32[]{:S(2)}, u32[]{:S(2)}) collective-permute-start(bf16[32,64,128]{2,1,0:T(8,128)(2,1)S(1)} %get-tuple-element.18), channel_id=1, source_target_pairs={{1,0},{2,1},{3,2},{4,3},{5,4},{6,5},{7,6},{9,8},{10,9},{11,10},{12... | collective-permute-start | bytes 1572872 | tf_op jit(solution)/shard_map/ppermute | solution.py:326
  14.5 38.3 %collective-permute-start.3 = (bf16[32,64,128]{2,1,0:T(8,128)(2,1)S(1)}, bf16[32,64,128]{2,1,0:T(8,128)(2,1)S(1)}, u32[]{:S(2)}, u32[]{:S(2)}) collective-permute-start(bf16[32,64,128]{2,1,0:T(8,128)(2,1)S(1)} %get-tuple-element.16), channel_id=1, source_target_pairs={{1,0},{2,1},{3,2},{4,3},{5,4},{6,5},{7,6},{9,8},{10,9},{11,10},{12... | collective-permute-start | bytes 1572872 | tf_op jit(solution)/shard_map/ppermute | solution.py:327
  16.4 17.9 %copy-start.4 = (s32[1024]{0:T(1024)S(1)}, s32[1024]{0:T(1024)}, u32[]{:S(2)}) copy-start(s32[1024]{0:T(1024)} %param.10) | copy-start | bytes 12292
  42.7 10.1 %copy-start = (bf16[32,64,128]{2,1,0:T(8,128)(2,1)}, bf16[32,64,128]{2,1,0:T(8,128)(2,1)S(1)}, u32[]{:S(2)}) copy-start(bf16[32,64,128]{2,1,0:T(8,128)(2,1)S(1)} %collective-permute-done.ulo_ref) | copy-start | bytes 1572868
  52.8 0.8 copy-start.1
  52.8 1.0 copy-start.2
  52.8 1.2 %copy-start.3 = (bf16[32,64,128]{2,1,0:T(8,128)(2,1)}, bf16[32,64,128]{2,1,0:T(8,128)(2,1)S(1)}, u32[]{:S(2)}) copy-start(bf16[32,64,128]{2,1,0:T(8,128)(2,1)S(1)} %collective-permute-done.3.khi_ref) | copy-start | bytes 1572868

commit v3 on v2

--- a/solution.py
+++ b/solution.py
@@ -74,87 +74,101 @@
 
 
 def border_kernel(
-    row_ref, col_ref, p_ref, u_ref, k_ref, ulo_ref, klo_ref, uhi_ref, khi_ref, turned_ref,
-    o_ref, picked_ref, scr, sem,
+    row_ref, col_ref, p_ref, u_ref, k_ref, turned_ref, ulo_ref, klo_ref, uhi_ref, khi_ref,
+    o_ref, picked_ref, scr, edge, u_own, k_own, sem,
 ):
-    g, e = pl.program_id(0), pl.program_id(1)
-    block, _, nx, ny = p_ref.shape
-    cells, members, _ = scr.shape
+    cells, members, ny = scr.shape
+    nx = edge.shape[2]
+    cz = cells // nx
+    last = cz - 1
+    tile = 16
+
+    def start(src, dst, i):
+        copy = pltpu.make_async_copy(src, dst, sem.at[i])
+        copy.start()
+        return copy
+
+    edges = [
+        [
+            start(p_ref.at[:, z], edge.at[e], 3 * e),
+            start(u_ref.at[:, z], u_own.at[e], 3 * e + 1),
+            start(k_ref.at[:, z], k_own.at[e], 3 * e + 2),
+        ]
+        for e, z in enumerate((0, last))
+    ]
     inner = pl.ds(nx, cells - 2 * nx)
-    load = pltpu.make_async_copy(turned_ref.at[inner], scr.at[inner], sem)
-    u = u_ref[:, 0].astype(jnp.float32)
-    k = k_ref[:, 0].astype(jnp.float32)
-    own = pl.ds(pl.multiple_of(g * block, block), block)
-
-    def fix(row, un_ref, kn_ref):
-        un = un_ref[...].astype(jnp.float32)
-        kn = kn_ref[...].astype(jnp.float32)
-        new = p_ref[:, 0] + half_step * (k + kn) * (un - u)
-        o_ref[:, 0] = new
-        for x in range(0, nx, 8):
-            scr[row + x : row + x + 8, own, :] = jnp.swapaxes(new[:, x : x + 8, :], 0, 1)
-
-    @pl.when(jnp.logical_and(g == 0, e == 0))
-    def _():
-        load.start()
-
-    @pl.when(e == 0)
-    def _():
-        fix(0, ulo_ref, klo_ref)
-
-    @pl.when(e == 1)
-    def _():
-        fix(cells - nx, uhi_ref, khi_ref)
-
-    @pl.when(jnp.logical_and(g == pl.num_programs(0) - 1, e == 1))
-    def _():
-        load.wait()
-        lane = lax.broadcasted_iota(jnp.int32, (members, ny), 1)
-        unroll = 8
-
-        def chunk(c, carry):
-            def step(s, acc):
-                for i in range(unroll):
-                    jj = s * unroll + i
-                    j = c * ny + jj
-                    v = pltpu.roll(scr[row_ref[j]], col_ref[j], 1)
-                    acc = jnp.where(lane == jj, v, acc)
-                return acc
-
-            zero = jnp.zeros((members, ny), jnp.float32)
-            acc = lax.fori_loop(0, ny // unroll, step, zero)
-            picked_ref[:, pl.ds(pl.multiple_of(c * ny, ny), ny)] = acc
+    load = start(turned_ref.at[inner], scr.at[inner], 6)
+    stores = []
+    for e, (z, un_ref, kn_ref) in enumerate(((0, ulo_ref, klo_ref), (last, uhi_ref, khi_ref))):
+        for copy in edges[e]:
+            copy.wait()
+
+        def fix(t, carry):
+            x = pl.multiple_of(t * tile, tile)
+            for m in range(0, members, 8):
+                at = (pl.ds(m, 8), pl.ds(x, tile), slice(None))
+                u = u_own[(e,) + at].astype(jnp.float32)
+                k = k_own[(e,) + at].astype(jnp.float32)
+                un = un_ref[at].astype(jnp.float32)
+                kn = kn_ref[at].astype(jnp.float32)
+                new = edge[(e,) + at] + half_step * (k + kn) * (un - u)
+                edge[(e,) + at] = new
+                for i in range(0, tile, 8):
+                    turned = jnp.swapaxes(new[:, i : i + 8, :], 0, 1)
+                    scr[pl.ds(z * nx + x + i, 8), m : m + 8, :] = turned
             return carry
 
-        lax.fori_loop(0, picked_ref.shape[1] // ny, chunk, 0)
+        lax.fori_loop(0, nx // tile, fix, 0)
+        stores.append(start(edge.at[e], o_ref.at[:, z], 7 + e))
+    load.wait()
+    lane = lax.broadcasted_iota(jnp.int32, (members, ny), 1)
+    unroll = 32
+
+    def chunk(c, carry):
+        def step(s, acc):
+            for i in range(unroll):
+                jj = s * unroll + i
+                j = c * ny + jj
+                v = pltpu.roll(scr[row_ref[j]], col_ref[j], 1)
+                acc = jnp.where(lane == jj, v, acc)
+            return acc
+
+        acc = lax.fori_loop(0, ny // unroll, step, jnp.zeros((members, ny), jnp.float32))
+        picked_ref[:, pl.ds(pl.multiple_of(c * ny, ny), ny)] = acc
+        return carry
+
+    lax.fori_loop(0, picked_ref.shape[1] // ny, chunk, 0)
+    for copy in stores:
+        copy.wait()
 
 
 def border(pred, turned, u, k, ulo, klo, uhi, khi, position):
     m, cz, nx, ny = u.shape
     slots = position.shape[0]
-    block = 8
     row = position // ny
     slot = jnp.arange(slots, dtype=jnp.int32)
     shift = (slot - position % ny) % ny
-    edge = pl.BlockSpec((block, 1, nx, ny), lambda g, e, *_: (g, e * (cz - 1), 0, 0))
-    halo = pl.BlockSpec((block, nx, ny), lambda g, e, *_: (g, 0, 0))
+    smem = pl.BlockSpec(memory_space=pltpu.SMEM)
+    vmem = pl.BlockSpec(memory_space=pltpu.VMEM)
+    whole = pl.BlockSpec(memory_space=pl.ANY)
     return pl.pallas_call(
         border_kernel,
-        grid_spec=pltpu.PrefetchScalarGridSpec(
-            num_scalar_prefetch=2,
-            grid=(m // block, 2),
-            in_specs=[edge, edge, edge, halo, halo, halo, halo]
-            + [pl.BlockSpec(memory_space=pl.ANY)],
-            out_specs=[edge, pl.BlockSpec((m, slots), lambda g, e, *_: (0, 0))],
-            scratch_shapes=[pltpu.VMEM(turned.shape, jnp.float32), pltpu.SemaphoreType.DMA],
-        ),
+        in_specs=[smem, smem] + [whole] * 4 + [vmem] * 4,
+        out_specs=[whole, vmem],
         out_shape=[
             jax.ShapeDtypeStruct(u.shape, jnp.float32),
             jax.ShapeDtypeStruct((m, slots), jnp.float32),
         ],
+        scratch_shapes=[
+            pltpu.VMEM(turned.shape, jnp.float32),
+            pltpu.VMEM((2, m, nx, ny), jnp.float32),
+            pltpu.VMEM((2, m, nx, ny), u.dtype),
+            pltpu.VMEM((2, m, nx, ny), u.dtype),
+            pltpu.SemaphoreType.DMA((9,)),
+        ],
         input_output_aliases={2: 0},
         name="border",
-    )(row, shift, pred, u, k, ulo, klo, uhi, khi, turned)
+    )(row, shift, pred, u, k, turned, ulo, klo, uhi, khi)
 
 
 def products_kernel(

time: 109 us -> 99.5 us (0.913)
  Pallas kernels: 72.4 us -> 63.1 us
    pallas_call x1, Pallas kernels: 22.8 us -> 13.6 us  [border(): pl.pallas_call(border_kernel, in_specs=[smem, smem] + [whole] * 4 + [vmem...]
  transfers between devices with their start and end apart: 4 -> 4, of which waited for: 2 -> 2; matrix products, arithmetic and copies ran while one was open for 3% -> 3% of each run, Pallas kernels for 16% -> 18%
where the time goes in v3:
time: 99.5 us; the launch traced here: 99.2 us
  Pallas kernels  63.1 us (63%)
  waiting for transfers between devices  17.9 us (18%)
  starting transfers between devices  10.9 us (11%)
  local copies, waits for them, and re-layouts  5.36 us (5%)
  between operations  1.36 us (1%)
    pallas_call x1, Pallas kernels, products(): pl.pallas_call(functools.partial(products_kernel, n_e, n_s), in_specs=[pl...  24 us
    pallas_call x1, Pallas kernels, stencil(): pl.pallas_call(stencil_kernel, grid=(m // block,), in_specs=[spec, spec],...  17.9 us
    pallas_call x1, Pallas kernels, border(): pl.pallas_call(border_kernel, in_specs=[smem, smem] + [whole] * 4 + [vmem...  13.6 us
    ppermute x1, waiting for transfers between devices, shards(): klo = lax.ppermute(k[:, -1], 'space', up)  10.1 us
    ppermute x1, waiting for transfers between devices, shards(): ulo = lax.ppermute(u[:, -1], 'space', up)  7.74 us
    pallas_call x1, Pallas kernels, update(): pl.pallas_call(update_kernel, out_shape=jax.ShapeDtypeStruct(params.shape...  7.68 us
    ppermute x1, starting transfers between devices, shards(): ulo = lax.ppermute(u[:, -1], 'space', up)  4.89 us
    ppermute x1, starting transfers between devices, shards(): klo = lax.ppermute(k[:, -1], 'space', up)  3.44 us
  transfers between devices with their start and end apart: 4, of which 2 were waited for; matrix products, arithmetic and copies ran while one was open for 3% of the time, Pallas kernels for 18%

profile of v3, /device:TPU:0, one launch (start us, length us, event | category | flops | bytes accessed | tf_op | source)
XLA Modules:
  0.0 99.2 jit_solution(6403578420909071734)
XLA Ops:
  0.6 2.1 %slice_bitcast_fusion.1 = (bf16[32,64,128]{2,1,0:T(8,128)(2,1)S(1)}, bf16[32,64,128]{2,1,0:T(8,128)(2,1)}) fusion(bf16[32,8,64,128]{3,2,1,0:T(8,128)(2,1)} %u_ref.3), kind=kLoop, calls=%fused_computation.1 | loop fusion | bytes 2097152 | tf_op jit(solution)/shard_map/squeeze | solution.py:340
  2.7 4.9 %collective-permute-start = (bf16[32,64,128]{2,1,0:T(8,128)(2,1)}, bf16[32,64,128]{2,1,0:T(8,128)(2,1)S(1)}, u32[]{:S(2)}, u32[]{:S(2)}) collective-permute-start(bf16[32,64,128]{2,1,0:T(8,128)(2,1)} %get-tuple-element.19), channel_id=1, source_target_pairs={{0,1},{1,2},{2,3},{3,4},{4,5},{5,6},{6,7},{8,9},{9,10},{10,11},{11... | collective-permute-start | bytes 1572872 | tf_op jit(solution)/shard_map/ppermute | solution.py:338
  7.6 2.1 %slice_bitcast_fusion = (bf16[32,64,128]{2,1,0:T(8,128)(2,1)S(1)}, bf16[32,64,128]{2,1,0:T(8,128)(2,1)}) fusion(bf16[32,8,64,128]{3,2,1,0:T(8,128)(2,1)} %k_ref.3), kind=kLoop, calls=%fused_computation | loop fusion | bytes 2097152 | tf_op jit(solution)/shard_map/squeeze | solution.py:341
  9.7 3.4 %collective-permute-start.1 = (bf16[32,64,128]{2,1,0:T(8,128)(2,1)}, bf16[32,64,128]{2,1,0:T(8,128)(2,1)S(1)}, u32[]{:S(2)}, u32[]{:S(2)}) collective-permute-start(bf16[32,64,128]{2,1,0:T(8,128)(2,1)} %get-tuple-element.17), channel_id=1, source_target_pairs={{0,1},{1,2},{2,3},{3,4},{4,5},{5,6},{6,7},{8,9},{9,10},{10,11},{11... | collective-permute-start | bytes 1572872 | tf_op jit(solution)/shard_map/ppermute | solution.py:339
  13.2 1.3 %collective-permute-start.2 = (bf16[32,64,128]{2,1,0:T(8,128)(2,1)S(1)}, bf16[32,64,128]{2,1,0:T(8,128)(2,1)S(1)}, u32[]{:S(2)}, u32[]{:S(2)}) collective-permute-start(bf16[32,64,128]{2,1,0:T(8,128)(2,1)S(1)} %get-tuple-element.18), channel_id=1, source_target_pairs={{1,0},{2,1},{3,2},{4,3},{5,4},{6,5},{7,6},{9,8},{10,9},{11,10},{12... | collective-permute-start | bytes 1572872 | tf_op jit(solution)/shard_map/ppermute | solution.py:340
  14.5 1.3 %collective-permute-start.3 = (bf16[32,64,128]{2,1,0:T(8,128)(2,1)S(1)}, bf16[32,64,128]{2,1,0:T(8,128)(2,1)S(1)}, u32[]{:S(2)}, u32[]{:S(2)}) collective-permute-start(bf16[32,64,128]{2,1,0:T(8,128)(2,1)S(1)} %get-tuple-element.16), channel_id=1, source_target_pairs={{1,0},{2,1},{3,2},{4,3},{5,4},{6,5},{7,6},{9,8},{10,9},{11,10},{12... | collective-permute-start | bytes 1572872 | tf_op jit(solution)/shard_map/ppermute | solution.py:341
  16.4 0.0 copy-start.4
  16.4 17.9 %stencil.1 = (f32[32,8,64,128]{3,2,1,0:T(8,128)}, f32[512,32,128]{2,1,0:T(8,128)}) custom-call(bf16[32,8,64,128]{3,2,1,0:T(8,128)(2,1)} %u_ref.3, bf16[32,8,64,128]{3,2,1,0:T(8,128)(2,1)} %k_ref.3), custom_call_target="tpu_custom_call" | custom-call | flops 83886080 | bytes 16777216 | tf_op jit(solution)/shard_map/stencil/pallas_call | solution.py:60
  34.3 0.0 copy-done.4
  34.3 0.6 add_select_fusion
  34.9 7.7 %collective-permute-done.ulo_ref = bf16[32,64,128]{2,1,0:T(8,128)(2,1)S(1)} collective-permute-done((bf16[32,64,128]{2,1,0:T(8,128)(2,1)}, bf16[32,64,128]{2,1,0:T(8,128)(2,1)S(1)}, u32[]{:S(2)}, u32[]{:S(2)}) %collective-permute-start) | collective-permute-done | bytes 524320 | tf_op jit(solution)/shard_map/ppermute | solution.py:338
  42.7 0.0 copy-start
  42.7 10.1 %collective-permute-done.1.klo_ref = bf16[32,64,128]{2,1,0:T(8,128)(2,1)S(1)} collective-permute-done((bf16[32,64,128]{2,1,0:T(8,128)(2,1)}, bf16[32,64,128]{2,1,0:T(8,128)(2,1)S(1)}, u32[]{:S(2)}, u32[]{:S(2)}) %collective-permute-start.1) | collective-permute-done | bytes 524320 | tf_op jit(solution)/shard_map/ppermute | solution.py:339
  52.8 0.0 copy-start.1
  52.8 0.0 collective-permute-done.2.uhi_ref
  52.8 0.0 copy-start.2
  52.8 0.0 collective-permute-done.3.khi_ref
  52.8 0.0 copy-start.3
  52.8 0.0 copy-done
  52.8 0.8 copy-done.1
  53.6 0.1 copy-done.2
  53.8 0.2 copy-done.3
  54.0 13.6 %border.1 = (f32[32,8,64,128]{3,2,1,0:T(8,128)}, f32[32,1024]{1,0:T(8,128)}) custom-call(s32[1024]{0:T(1024)} %get-tuple-element.21.row_ref, s32[1024]{0:T(1024)} %get-tuple-element.20.col_ref, f32[32,8,64,128]{3,2,1,0:T(8,128)} %get-tuple-element.9.p_ref, bf16[32,8,64,128]{3,2,1,0:T(8,128)(2,1)} %u_ref.3, ...), custom_call_target="tpu_custom_call", output_to_operand_aliasing={{0}: (2, {})} | custom-call | tf_op jit(solution)/shard_map/border/pallas_call | solution.py:154
  67.5 24.0 %products.1 = (f32[4,32,128]{2,1,0:T(8,128)}, f32[32,128]{1,0:T(8,128)}, f32[4,32,256]{2,1,0:T(8,128)}) custom-call(s32[1]{0:T(128)S(6)} %copy.20.count_ref, f32[32,1024]{1,0:T(8,128)} %get-tuple-element.11.picked_ref, f32[32,1024]{1,0:T(8,128)} %noise_ref.1, f32[1,1024]{1,0:T(1,128)} %bitcast.22, f32[1,1024]{1,0:T(1,128)} %bitcast.23, f32[32,256]{1,0:T(8,128)} %params_ref.3), custom_call_target="tpu_custom_call" | custom-call | tf_op jit(solution)/shard_map/products/pallas_call | solution.py:255
  91.5 7.7 %update.1 = f32[32,256]{1,0:T(8,128)} custom-call(f32[128,128]{1,0:T(8,128)} %bitcast.21, f32[32,128]{1,0:T(8,128)} %get-tuple-element.13.cross_ref, f32[128,256]{1,0:T(8,128)} %bitcast.20, f32[32,256]{1,0:T(8,128)} %params_ref.3), custom_call_target="tpu_custom_call" | custom-call | tf_op jit(solution)/shard_map/update/pallas_call | solution.py:327
Async XLA Ops:
  2.7 39.9 %collective-permute-start = (bf16[32,64,128]{2,1,0:T(8,128)(2,1)}, bf16[32,64,128]{2,1,0:T(8,128)(2,1)S(1)}, u32[]{:S(2)}, u32[]{:S(2)}) collective-permute-start(bf16[32,64,128]{2,1,0:T(8,128)(2,1)} %get-tuple-element.19), channel_id=1, source_target_pairs={{0,1},{1,2},{2,3},{3,4},{4,5},{5,6},{6,7},{8,9},{9,10},{10,11},{11... | collective-permute-start | bytes 1572872 | tf_op jit(solution)/shard_map/ppermute | solution.py:338
  9.7 43.0 %collective-permute-start.1 = (bf16[32,64,128]{2,1,0:T(8,128)(2,1)}, bf16[32,64,128]{2,1,0:T(8,128)(2,1)S(1)}, u32[]{:S(2)}, u32[]{:S(2)}) collective-permute-start(bf16[32,64,128]{2,1,0:T(8,128)(2,1)} %get-tuple-element.17), channel_id=1, source_target_pairs={{0,1},{1,2},{2,3},{3,4},{4,5},{5,6},{6,7},{8,9},{9,10},{10,11},{11... | collective-permute-start | bytes 1572872 | tf_op jit(solution)/shard_map/ppermute | solution.py:339
  13.2 39.6 %collective-permute-start.2 = (bf16[32,64,128]{2,1,0:T(8,128)(2,1)S(1)}, bf16[32,64,128]{2,1,0:T(8,128)(2,1)S(1)}, u32[]{:S(2)}, u32[]{:S(2)}) collective-permute-start(bf16[32,64,128]{2,1,0:T(8,128)(2,1)S(1)} %get-tuple-element.18), channel_id=1, source_target_pairs={{1,0},{2,1},{3,2},{4,3},{5,4},{6,5},{7,6},{9,8},{10,9},{11,10},{12... | collective-permute-start | bytes 1572872 | tf_op jit(solution)/shard_map/ppermute | solution.py:340
  14.5 38.3 %collective-permute-start.3 = (bf16[32,64,128]{2,1,0:T(8,128)(2,1)S(1)}, bf16[32,64,128]{2,1,0:T(8,128)(2,1)S(1)}, u32[]{:S(2)}, u32[]{:S(2)}) collective-permute-start(bf16[32,64,128]{2,1,0:T(8,128)(2,1)S(1)} %get-tuple-element.16), channel_id=1, source_target_pairs={{1,0},{2,1},{3,2},{4,3},{5,4},{6,5},{7,6},{9,8},{10,9},{11,10},{12... | collective-permute-start | bytes 1572872 | tf_op jit(solution)/shard_map/ppermute | solution.py:341
  16.4 17.9 %copy-start.4 = (s32[1024]{0:T(1024)S(1)}, s32[1024]{0:T(1024)}, u32[]{:S(2)}) copy-start(s32[1024]{0:T(1024)} %param.10) | copy-start | bytes 12292
  42.7 10.1 %copy-start = (bf16[32,64,128]{2,1,0:T(8,128)(2,1)}, bf16[32,64,128]{2,1,0:T(8,128)(2,1)S(1)}, u32[]{:S(2)}) copy-start(bf16[32,64,128]{2,1,0:T(8,128)(2,1)S(1)} %collective-permute-done.ulo_ref) | copy-start | bytes 1572868
  52.8 0.8 copy-start.1
  52.8 1.0 copy-start.2
  52.8 1.2 %copy-start.3 = (bf16[32,64,128]{2,1,0:T(8,128)(2,1)}, bf16[32,64,128]{2,1,0:T(8,128)(2,1)S(1)}, u32[]{:S(2)}) copy-start(bf16[32,64,128]{2,1,0:T(8,128)(2,1)S(1)} %collective-permute-done.3.khi_ref) | copy-start | bytes 1572868

commit v4 on v3

--- a/solution.py
+++ b/solution.py
@@ -175,7 +175,7 @@
     n_e, n_s, count_ref, picked_ref, noise_ref, values_ref, std_ref, params_ref,
     gram_ref, cross_ref, all_params_ref,
     all_picked, part, parts, total,
-    send_a, recv_a, send_p, recv_p, send_s, recv_s, send_g, recv_g,
+    send_a, recv_a, send_h, recv_h, send_p, recv_p, send_s, recv_s, send_g, recv_g,
 ):
     own, slots = picked_ref.shape
     members = own * n_e
@@ -203,9 +203,13 @@
         copy.start()
         return copy
 
+    pair = me_e + 1 - 2 * lax.rem(me_e, 2)
+    partner = (pair, me_s)
+    hops = n_e // 2
+    handed = [send(picked_ref, all_picked.at[me_e], send_h.at[0], recv_h.at[0], partner)]
     picked_copies = [
-        send(picked_ref, all_picked.at[me_e], send_a.at[d], recv_a.at[d], ens_peer(d))
-        for d in range(1, n_e)
+        send(picked_ref, all_picked.at[me_e], send_a.at[d], recv_a.at[d], ens_peer(2 * d))
+        for d in range(1, hops)
     ]
     params_copies = [
         send(params_ref, all_params_ref.at[me_e], send_p.at[d], recv_p.at[d], ens_peer(d))
@@ -218,7 +222,11 @@
     std = std_ref[...]
     inverse = jnp.where(live, 1.0 / (std * scale), 0.0)
     misfit = jnp.where(live, (values_ref[...] - mine) / std + noise_ref[...], 0.0)
-    for copy in picked_copies:
+    for d in range(1, hops):
+        picked_copies[d - 1].wait()
+        block = all_picked.at[lax.rem(me_e + n_e - 2 * d, n_e)]
+        handed.append(send(block, block, send_h.at[d], recv_h.at[d], partner))
+    for copy in handed:
         copy.wait()
     everyone = all_picked[...].reshape(members, slots)
     centre = jnp.sum(everyone, axis=0, keepdims=True) / members
@@ -267,7 +275,7 @@
             pltpu.VMEM((n_s, 2 * own, n_e * own), jnp.float32),
             pltpu.VMEM((own, n_e * own), jnp.float32),
         ]
-        + [dma((n_e,))] * 4 + [dma((n_s,))] * 2 + [dma((n_e,))] * 2,
+        + [dma((n_e,))] * 6 + [dma((n_s,))] * 2 + [dma((n_e,))] * 2,
         compiler_params=pltpu.CompilerParams(collective_id=0, has_side_effects=True),
         name="products",
     )(count, picked, noise, values.reshape(1, -1), std.reshape(1, -1), params)
@@ -282,11 +290,13 @@
     work[:members] = gram_ref[...] + jnp.where(rows == cols, 1.0, 0.0)
     work[members:] = cross_ref[...]
 
-    pivots = 4
-
-    def step(s, diagonal):
-        first = s * pivots
-        t = work[...]
+    pivots = 8
+    segments = 4
+    span = members // segments
+
+    def step(lo, s, diagonal):
+        first = lo + s * pivots
+        t = work[lo:]
         here = [lane == first + i for i in range(pivots)]
         columns = [
             jnp.sum(jnp.where(here[i], t, 0.0), axis=1, keepdims=True) for i in range(pivots)
@@ -308,11 +318,14 @@
                 rows[j] = rows[j] - corner[j][i] * factor
                 for l in range(i + 1, pivots):
                     corner[l][j] = corner[l][j] - corner[l][i] * ratio
-        work[...] = t
+        work[lo:] = t
         return diagonal
 
-    ones = jnp.ones((1, members), jnp.float32)
-    diagonal = lax.fori_loop(0, members // pivots, step, ones)
+    diagonal = jnp.ones((1, members), jnp.float32)
+    for part in range(segments):
+        diagonal = lax.fori_loop(
+            0, span // pivots, functools.partial(step, part * span), diagonal
+        )
     weights = work[members:] / diagonal
     all_params = all_params_ref[...]
     centre = jnp.sum(all_params, axis=0, keepdims=True) / members

time: 99.5 us -> 98.4 us (0.989)
  Pallas kernels: 63.1 us -> 61.9 us
    pallas_call x1, Pallas kernels: 24 us -> 22.9 us  [products(): pl.pallas_call(functools.partial(products_kernel, n_e, n_s), in_specs=[pl...]
where the time goes in v4:
time: 98.4 us; the launch traced here: 98 us
  Pallas kernels  61.9 us (63%)
  waiting for transfers between devices  17.8 us (18%)
  starting transfers between devices  10.9 us (11%)
  local copies, waits for them, and re-layouts  5.36 us (5%)
  between operations  1.36 us (1%)
    pallas_call x1, Pallas kernels, products(): pl.pallas_call(functools.partial(products_kernel, n_e, n_s), in_specs=[pl...  22.9 us
    pallas_call x1, Pallas kernels, stencil(): pl.pallas_call(stencil_kernel, grid=(m // block,), in_specs=[spec, spec],...  17.9 us
    pallas_call x1, Pallas kernels, border(): pl.pallas_call(border_kernel, in_specs=[smem, smem] + [whole] * 4 + [vmem...  13.6 us
    ppermute x1, waiting for transfers between devices, shards(): klo = lax.ppermute(k[:, -1], 'space', up)  10.1 us
    ppermute x1, waiting for transfers between devices, shards(): ulo = lax.ppermute(u[:, -1], 'space', up)  7.74 us
    pallas_call x1, Pallas kernels, update(): pl.pallas_call(update_kernel, out_shape=jax.ShapeDtypeStruct(params.shape...  7.63 us
    ppermute x1, starting transfers between devices, shards(): ulo = lax.ppermute(u[:, -1], 'space', up)  4.89 us
    ppermute x1, starting transfers between devices, shards(): klo = lax.ppermute(k[:, -1], 'space', up)  3.44 us
  transfers between devices with their start and end apart: 4, of which 2 were waited for; matrix products, arithmetic and copies ran while one was open for 3% of the time, Pallas kernels for 18%

profile of v4, /device:TPU:0, one launch (start us, length us, event | category | flops | bytes accessed | tf_op | source)
XLA Modules:
  0.0 98.0 jit_solution(3079001358749432743)
XLA Ops:
  0.6 2.1 %slice_bitcast_fusion.1 = (bf16[32,64,128]{2,1,0:T(8,128)(2,1)S(1)}, bf16[32,64,128]{2,1,0:T(8,128)(2,1)}) fusion(bf16[32,8,64,128]{3,2,1,0:T(8,128)(2,1)} %u_ref.3), kind=kLoop, calls=%fused_computation.1 | loop fusion | bytes 2097152 | tf_op jit(solution)/shard_map/squeeze | solution.py:353
  2.7 4.9 %collective-permute-start = (bf16[32,64,128]{2,1,0:T(8,128)(2,1)}, bf16[32,64,128]{2,1,0:T(8,128)(2,1)S(1)}, u32[]{:S(2)}, u32[]{:S(2)}) collective-permute-start(bf16[32,64,128]{2,1,0:T(8,128)(2,1)} %get-tuple-element.19), channel_id=1, source_target_pairs={{0,1},{1,2},{2,3},{3,4},{4,5},{5,6},{6,7},{8,9},{9,10},{10,11},{11... | collective-permute-start | bytes 1572872 | tf_op jit(solution)/shard_map/ppermute | solution.py:351
  7.6 2.1 %slice_bitcast_fusion = (bf16[32,64,128]{2,1,0:T(8,128)(2,1)S(1)}, bf16[32,64,128]{2,1,0:T(8,128)(2,1)}) fusion(bf16[32,8,64,128]{3,2,1,0:T(8,128)(2,1)} %k_ref.3), kind=kLoop, calls=%fused_computation | loop fusion | bytes 2097152 | tf_op jit(solution)/shard_map/squeeze | solution.py:354
  9.7 3.4 %collective-permute-start.1 = (bf16[32,64,128]{2,1,0:T(8,128)(2,1)}, bf16[32,64,128]{2,1,0:T(8,128)(2,1)S(1)}, u32[]{:S(2)}, u32[]{:S(2)}) collective-permute-start(bf16[32,64,128]{2,1,0:T(8,128)(2,1)} %get-tuple-element.17), channel_id=1, source_target_pairs={{0,1},{1,2},{2,3},{3,4},{4,5},{5,6},{6,7},{8,9},{9,10},{10,11},{11... | collective-permute-start | bytes 1572872 | tf_op jit(solution)/shard_map/ppermute | solution.py:352
  13.2 1.3 %collective-permute-start.2 = (bf16[32,64,128]{2,1,0:T(8,128)(2,1)S(1)}, bf16[32,64,128]{2,1,0:T(8,128)(2,1)S(1)}, u32[]{:S(2)}, u32[]{:S(2)}) collective-permute-start(bf16[32,64,128]{2,1,0:T(8,128)(2,1)S(1)} %get-tuple-element.18), channel_id=1, source_target_pairs={{1,0},{2,1},{3,2},{4,3},{5,4},{6,5},{7,6},{9,8},{10,9},{11,10},{12... | collective-permute-start | bytes 1572872 | tf_op jit(solution)/shard_map/ppermute | solution.py:353
  14.5 1.3 %collective-permute-start.3 = (bf16[32,64,128]{2,1,0:T(8,128)(2,1)S(1)}, bf16[32,64,128]{2,1,0:T(8,128)(2,1)S(1)}, u32[]{:S(2)}, u32[]{:S(2)}) collective-permute-start(bf16[32,64,128]{2,1,0:T(8,128)(2,1)S(1)} %get-tuple-element.16), channel_id=1, source_target_pairs={{1,0},{2,1},{3,2},{4,3},{5,4},{6,5},{7,6},{9,8},{10,9},{11,10},{12... | collective-permute-start | bytes 1572872 | tf_op jit(solution)/shard_map/ppermute | solution.py:354
  16.4 0.0 copy-start.4
  16.4 17.9 %stencil.1 = (f32[32,8,64,128]{3,2,1,0:T(8,128)}, f32[512,32,128]{2,1,0:T(8,128)}) custom-call(bf16[32,8,64,128]{3,2,1,0:T(8,128)(2,1)} %u_ref.3, bf16[32,8,64,128]{3,2,1,0:T(8,128)(2,1)} %k_ref.3), custom_call_target="tpu_custom_call" | custom-call | flops 83886080 | bytes 16777216 | tf_op jit(solution)/shard_map/stencil/pallas_call | solution.py:60
  34.3 0.0 copy-done.4
  34.3 0.6 add_select_fusion
  34.9 7.7 %collective-permute-done.ulo_ref = bf16[32,64,128]{2,1,0:T(8,128)(2,1)S(1)} collective-permute-done((bf16[32,64,128]{2,1,0:T(8,128)(2,1)}, bf16[32,64,128]{2,1,0:T(8,128)(2,1)S(1)}, u32[]{:S(2)}, u32[]{:S(2)}) %collective-permute-start) | collective-permute-done | bytes 524320 | tf_op jit(solution)/shard_map/ppermute | solution.py:351
  42.7 0.0 copy-start
  42.7 10.1 %collective-permute-done.1.klo_ref = bf16[32,64,128]{2,1,0:T(8,128)(2,1)S(1)} collective-permute-done((bf16[32,64,128]{2,1,0:T(8,128)(2,1)}, bf16[32,64,128]{2,1,0:T(8,128)(2,1)S(1)}, u32[]{:S(2)}, u32[]{:S(2)}) %collective-permute-start.1) | collective-permute-done | bytes 524320 | tf_op jit(solution)/shard_map/ppermute | solution.py:352
  52.8 0.0 copy-start.1
  52.8 0.0 collective-permute-done.2.uhi_ref
  52.8 0.0 copy-start.2
  52.8 0.0 collective-permute-done.3.khi_ref
  52.8 0.0 copy-start.3
  52.8 0.0 copy-done
  52.8 0.8 copy-done.1
  53.6 0.1 copy-done.2
  53.8 0.2 copy-done.3
  54.0 13.6 %border.1 = (f32[32,8,64,128]{3,2,1,0:T(8,128)}, f32[32,1024]{1,0:T(8,128)}) custom-call(s32[1024]{0:T(1024)} %get-tuple-element.21.row_ref, s32[1024]{0:T(1024)} %get-tuple-element.20.col_ref, f32[32,8,64,128]{3,2,1,0:T(8,128)} %get-tuple-element.9.p_ref, bf16[32,8,64,128]{3,2,1,0:T(8,128)(2,1)} %u_ref.3, ...), custom_call_target="tpu_custom_call", output_to_operand_aliasing={{0}: (2, {})} | custom-call | tf_op jit(solution)/shard_map/border/pallas_call | solution.py:154
  67.5 22.9 %products.1 = (f32[4,32,128]{2,1,0:T(8,128)}, f32[32,128]{1,0:T(8,128)}, f32[4,32,256]{2,1,0:T(8,128)}) custom-call(s32[1]{0:T(128)S(6)} %copy.20.count_ref, f32[32,1024]{1,0:T(8,128)} %get-tuple-element.11.picked_ref, f32[32,1024]{1,0:T(8,128)} %noise_ref.1, f32[1,1024]{1,0:T(1,128)} %bitcast.22, f32[1,1024]{1,0:T(1,128)} %bitcast.23, f32[32,256]{1,0:T(8,128)} %params_ref.3), custom_call_target="tpu_custom_call" | custom-call | tf_op jit(solution)/shard_map/products/pallas_call | solution.py:263
  90.4 7.6 %update.1 = f32[32,256]{1,0:T(8,128)} custom-call(f32[128,128]{1,0:T(8,128)} %bitcast.21, f32[32,128]{1,0:T(8,128)} %get-tuple-element.13.cross_ref, f32[128,256]{1,0:T(8,128)} %bitcast.20, f32[32,256]{1,0:T(8,128)} %params_ref.3), custom_call_target="tpu_custom_call" | custom-call | tf_op jit(solution)/shard_map/update/pallas_call | solution.py:340
Async XLA Ops:
  2.7 39.9 %collective-permute-start = (bf16[32,64,128]{2,1,0:T(8,128)(2,1)}, bf16[32,64,128]{2,1,0:T(8,128)(2,1)S(1)}, u32[]{:S(2)}, u32[]{:S(2)}) collective-permute-start(bf16[32,64,128]{2,1,0:T(8,128)(2,1)} %get-tuple-element.19), channel_id=1, source_target_pairs={{0,1},{1,2},{2,3},{3,4},{4,5},{5,6},{6,7},{8,9},{9,10},{10,11},{11... | collective-permute-start | bytes 1572872 | tf_op jit(solution)/shard_map/ppermute | solution.py:351
  9.7 43.0 %collective-permute-start.1 = (bf16[32,64,128]{2,1,0:T(8,128)(2,1)}, bf16[32,64,128]{2,1,0:T(8,128)(2,1)S(1)}, u32[]{:S(2)}, u32[]{:S(2)}) collective-permute-start(bf16[32,64,128]{2,1,0:T(8,128)(2,1)} %get-tuple-element.17), channel_id=1, source_target_pairs={{0,1},{1,2},{2,3},{3,4},{4,5},{5,6},{6,7},{8,9},{9,10},{10,11},{11... | collective-permute-start | bytes 1572872 | tf_op jit(solution)/shard_map/ppermute | solution.py:352
  13.2 39.6 %collective-permute-start.2 = (bf16[32,64,128]{2,1,0:T(8,128)(2,1)S(1)}, bf16[32,64,128]{2,1,0:T(8,128)(2,1)S(1)}, u32[]{:S(2)}, u32[]{:S(2)}) collective-permute-start(bf16[32,64,128]{2,1,0:T(8,128)(2,1)S(1)} %get-tuple-element.18), channel_id=1, source_target_pairs={{1,0},{2,1},{3,2},{4,3},{5,4},{6,5},{7,6},{9,8},{10,9},{11,10},{12... | collective-permute-start | bytes 1572872 | tf_op jit(solution)/shard_map/ppermute | solution.py:353
  14.5 38.3 %collective-permute-start.3 = (bf16[32,64,128]{2,1,0:T(8,128)(2,1)S(1)}, bf16[32,64,128]{2,1,0:T(8,128)(2,1)S(1)}, u32[]{:S(2)}, u32[]{:S(2)}) collective-permute-start(bf16[32,64,128]{2,1,0:T(8,128)(2,1)S(1)} %get-tuple-element.16), channel_id=1, source_target_pairs={{1,0},{2,1},{3,2},{4,3},{5,4},{6,5},{7,6},{9,8},{10,9},{11,10},{12... | collective-permute-start | bytes 1572872 | tf_op jit(solution)/shard_map/ppermute | solution.py:354
  16.4 17.9 %copy-start.4 = (s32[1024]{0:T(1024)S(1)}, s32[1024]{0:T(1024)}, u32[]{:S(2)}) copy-start(s32[1024]{0:T(1024)} %param.10) | copy-start | bytes 12292
  42.7 10.1 %copy-start = (bf16[32,64,128]{2,1,0:T(8,128)(2,1)}, bf16[32,64,128]{2,1,0:T(8,128)(2,1)S(1)}, u32[]{:S(2)}) copy-start(bf16[32,64,128]{2,1,0:T(8,128)(2,1)S(1)} %collective-permute-done.ulo_ref) | copy-start | bytes 1572868
  52.8 0.8 copy-start.1
  52.8 1.0 copy-start.2
  52.8 1.2 %copy-start.3 = (bf16[32,64,128]{2,1,0:T(8,128)(2,1)}, bf16[32,64,128]{2,1,0:T(8,128)(2,1)S(1)}, u32[]{:S(2)}) copy-start(bf16[32,64,128]{2,1,0:T(8,128)(2,1)S(1)} %collective-permute-done.3.khi_ref) | copy-start | bytes 1572868

commit v5 on v4

--- a/solution.py
+++ b/solution.py
@@ -174,7 +174,7 @@
 def products_kernel(
     n_e, n_s, count_ref, picked_ref, noise_ref, values_ref, std_ref, params_ref,
     gram_ref, cross_ref, all_params_ref,
-    all_picked, part, parts, total,
+    all_picked, part, paired, parts, total,
     send_a, recv_a, send_h, recv_h, send_p, recv_p, send_s, recv_s, send_g, recv_g,
 ):
     own, slots = picked_ref.shape
@@ -191,9 +191,11 @@
     barrier = pltpu.get_barrier_semaphore()
     for d in range(1, n_e):
         pl.semaphore_signal(barrier, inc=1, device_id=ens_peer(d), device_id_type=MESH)
-    for d in range(1, n_s):
-        pl.semaphore_signal(barrier, inc=1, device_id=space_peer(d), device_id_type=MESH)
-    pl.semaphore_wait(barrier, n_e + n_s - 2)
+    space_pair = (me_e, me_s + 1 - 2 * lax.rem(me_s, 2))
+    pl.semaphore_signal(barrier, inc=1, device_id=space_pair, device_id_type=MESH)
+    for d in range(1, n_s // 2):
+        pl.semaphore_signal(barrier, inc=1, device_id=space_peer(2 * d), device_id_type=MESH)
+    pl.semaphore_wait(barrier, n_e - 1 + n_s // 2)
 
     def send(src, dst, ssem, rsem, peer):
         copy = pltpu.make_async_remote_copy(
@@ -236,11 +238,14 @@
         left, spread, (((1,), (1,)), ((), ())),
         precision=HI, preferred_element_type=jnp.float32,
     )
+    send(part, parts.at[0], send_s.at[0], recv_s.at[0], space_pair).wait()
+    acc = part[...] + parts[0]
+    paired[...] = acc
     space_copies = [
-        send(part, parts.at[d], send_s.at[d], recv_s.at[d], space_peer(d)) for d in range(1, n_s)
-    ]
-    acc = part[...]
-    for d in range(1, n_s):
+        send(paired, parts.at[d], send_s.at[d], recv_s.at[d], space_peer(2 * d))
+        for d in range(1, n_s // 2)
+    ]
+    for d in range(1, n_s // 2):
         space_copies[d - 1].wait()
         acc += parts[d]
     total[...] = acc[:own]
@@ -272,7 +277,8 @@
         scratch_shapes=[
             pltpu.VMEM((n_e, own, slots), jnp.float32),
             pltpu.VMEM((2 * own, n_e * own), jnp.float32),
-            pltpu.VMEM((n_s, 2 * own, n_e * own), jnp.float32),
+            pltpu.VMEM((2 * own, n_e * own), jnp.float32),
+            pltpu.VMEM((n_s // 2, 2 * own, n_e * own), jnp.float32),
             pltpu.VMEM((own, n_e * own), jnp.float32),
         ]
         + [dma((n_e,))] * 6 + [dma((n_s,))] * 2 + [dma((n_e,))] * 2,

time: 98.4 us -> 98.9 us (level)
  no operation moved by 1% of the time
where the time goes in v5:
time: 98.9 us; the launch traced here: 98.5 us
  Pallas kernels  62.4 us (63%)
  waiting for transfers between devices  17.8 us (18%)
  starting transfers between devices  10.9 us (11%)
  local copies, waits for them, and re-layouts  5.36 us (5%)
  between operations  1.36 us (1%)
    pallas_call x1, Pallas kernels, products(): pl.pallas_call(functools.partial(products_kernel, n_e, n_s), in_specs=[pl...  23.4 us
    pallas_call x1, Pallas kernels, stencil(): pl.pallas_call(stencil_kernel, grid=(m // block,), in_specs=[spec, spec],...  17.9 us
    pallas_call x1, Pallas kernels, border(): pl.pallas_call(border_kernel, in_specs=[smem, smem] + [whole] * 4 + [vmem...  13.6 us
    ppermute x1, waiting for transfers between devices, shards(): klo = lax.ppermute(k[:, -1], 'space', up)  10.1 us
    ppermute x1, waiting for transfers between devices, shards(): ulo = lax.ppermute(u[:, -1], 'space', up)  7.74 us
    pallas_call x1, Pallas kernels, update(): pl.pallas_call(update_kernel, out_shape=jax.ShapeDtypeStruct(params.shape...  7.63 us
    ppermute x1, starting transfers between devices, shards(): ulo = lax.ppermute(u[:, -1], 'space', up)  4.89 us
    ppermute x1, starting transfers between devices, shards(): klo = lax.ppermute(k[:, -1], 'space', up)  3.44 us
  transfers between devices with their start and end apart: 4, of which 2 were waited for; matrix products, arithmetic and copies ran while one was open for 3% of the time, Pallas kernels for 18%

profile of v5, /device:TPU:0, one launch (start us, length us, event | category | flops | bytes accessed | tf_op | source)
XLA Modules:
  0.0 98.5 jit_solution(9822890705695261852)
XLA Ops:
  0.6 2.1 %slice_bitcast_fusion.1 = (bf16[32,64,128]{2,1,0:T(8,128)(2,1)S(1)}, bf16[32,64,128]{2,1,0:T(8,128)(2,1)}) fusion(bf16[32,8,64,128]{3,2,1,0:T(8,128)(2,1)} %u_ref.3), kind=kLoop, calls=%fused_computation.1 | loop fusion | bytes 2097152 | tf_op jit(solution)/shard_map/squeeze | solution.py:359
  2.7 4.9 %collective-permute-start = (bf16[32,64,128]{2,1,0:T(8,128)(2,1)}, bf16[32,64,128]{2,1,0:T(8,128)(2,1)S(1)}, u32[]{:S(2)}, u32[]{:S(2)}) collective-permute-start(bf16[32,64,128]{2,1,0:T(8,128)(2,1)} %get-tuple-element.19), channel_id=1, source_target_pairs={{0,1},{1,2},{2,3},{3,4},{4,5},{5,6},{6,7},{8,9},{9,10},{10,11},{11... | collective-permute-start | bytes 1572872 | tf_op jit(solution)/shard_map/ppermute | solution.py:357
  7.6 2.1 %slice_bitcast_fusion = (bf16[32,64,128]{2,1,0:T(8,128)(2,1)S(1)}, bf16[32,64,128]{2,1,0:T(8,128)(2,1)}) fusion(bf16[32,8,64,128]{3,2,1,0:T(8,128)(2,1)} %k_ref.3), kind=kLoop, calls=%fused_computation | loop fusion | bytes 2097152 | tf_op jit(solution)/shard_map/squeeze | solution.py:360
  9.7 3.4 %collective-permute-start.1 = (bf16[32,64,128]{2,1,0:T(8,128)(2,1)}, bf16[32,64,128]{2,1,0:T(8,128)(2,1)S(1)}, u32[]{:S(2)}, u32[]{:S(2)}) collective-permute-start(bf16[32,64,128]{2,1,0:T(8,128)(2,1)} %get-tuple-element.17), channel_id=1, source_target_pairs={{0,1},{1,2},{2,3},{3,4},{4,5},{5,6},{6,7},{8,9},{9,10},{10,11},{11... | collective-permute-start | bytes 1572872 | tf_op jit(solution)/shard_map/ppermute | solution.py:358
  13.2 1.3 %collective-permute-start.2 = (bf16[32,64,128]{2,1,0:T(8,128)(2,1)S(1)}, bf16[32,64,128]{2,1,0:T(8,128)(2,1)S(1)}, u32[]{:S(2)}, u32[]{:S(2)}) collective-permute-start(bf16[32,64,128]{2,1,0:T(8,128)(2,1)S(1)} %get-tuple-element.18), channel_id=1, source_target_pairs={{1,0},{2,1},{3,2},{4,3},{5,4},{6,5},{7,6},{9,8},{10,9},{11,10},{12... | collective-permute-start | bytes 1572872 | tf_op jit(solution)/shard_map/ppermute | solution.py:359
  14.5 1.3 %collective-permute-start.3 = (bf16[32,64,128]{2,1,0:T(8,128)(2,1)S(1)}, bf16[32,64,128]{2,1,0:T(8,128)(2,1)S(1)}, u32[]{:S(2)}, u32[]{:S(2)}) collective-permute-start(bf16[32,64,128]{2,1,0:T(8,128)(2,1)S(1)} %get-tuple-element.16), channel_id=1, source_target_pairs={{1,0},{2,1},{3,2},{4,3},{5,4},{6,5},{7,6},{9,8},{10,9},{11,10},{12... | collective-permute-start | bytes 1572872 | tf_op jit(solution)/shard_map/ppermute | solution.py:360
  16.4 0.0 copy-start.4
  16.4 17.9 %stencil.1 = (f32[32,8,64,128]{3,2,1,0:T(8,128)}, f32[512,32,128]{2,1,0:T(8,128)}) custom-call(bf16[32,8,64,128]{3,2,1,0:T(8,128)(2,1)} %u_ref.3, bf16[32,8,64,128]{3,2,1,0:T(8,128)(2,1)} %k_ref.3), custom_call_target="tpu_custom_call" | custom-call | flops 83886080 | bytes 16777216 | tf_op jit(solution)/shard_map/stencil/pallas_call | solution.py:60
  34.3 0.0 copy-done.4
  34.3 0.6 add_select_fusion
  34.9 7.7 %collective-permute-done.ulo_ref = bf16[32,64,128]{2,1,0:T(8,128)(2,1)S(1)} collective-permute-done((bf16[32,64,128]{2,1,0:T(8,128)(2,1)}, bf16[32,64,128]{2,1,0:T(8,128)(2,1)S(1)}, u32[]{:S(2)}, u32[]{:S(2)}) %collective-permute-start) | collective-permute-done | bytes 524320 | tf_op jit(solution)/shard_map/ppermute | solution.py:357
  42.7 0.0 copy-start
  42.7 10.1 %collective-permute-done.1.klo_ref = bf16[32,64,128]{2,1,0:T(8,128)(2,1)S(1)} collective-permute-done((bf16[32,64,128]{2,1,0:T(8,128)(2,1)}, bf16[32,64,128]{2,1,0:T(8,128)(2,1)S(1)}, u32[]{:S(2)}, u32[]{:S(2)}) %collective-permute-start.1) | collective-permute-done | bytes 524320 | tf_op jit(solution)/shard_map/ppermute | solution.py:358
  52.8 0.0 copy-start.1
  52.8 0.0 collective-permute-done.2.uhi_ref
  52.8 0.0 copy-start.2
  52.8 0.0 collective-permute-done.3.khi_ref
  52.8 0.0 copy-start.3
  52.8 0.0 copy-done
  52.8 0.8 copy-done.1
  53.6 0.1 copy-done.2
  53.8 0.2 copy-done.3
  54.0 13.6 %border.1 = (f32[32,8,64,128]{3,2,1,0:T(8,128)}, f32[32,1024]{1,0:T(8,128)}) custom-call(s32[1024]{0:T(1024)} %get-tuple-element.21.row_ref, s32[1024]{0:T(1024)} %get-tuple-element.20.col_ref, f32[32,8,64,128]{3,2,1,0:T(8,128)} %get-tuple-element.9.p_ref, bf16[32,8,64,128]{3,2,1,0:T(8,128)(2,1)} %u_ref.3, ...), custom_call_target="tpu_custom_call", output_to_operand_aliasing={{0}: (2, {})} | custom-call | tf_op jit(solution)/shard_map/border/pallas_call | solution.py:154
  67.5 23.4 %products.1 = (f32[4,32,128]{2,1,0:T(8,128)}, f32[32,128]{1,0:T(8,128)}, f32[4,32,256]{2,1,0:T(8,128)}) custom-call(s32[1]{0:T(128)S(6)} %copy.20.count_ref, f32[32,1024]{1,0:T(8,128)} %get-tuple-element.11.picked_ref, f32[32,1024]{1,0:T(8,128)} %noise_ref.1, f32[1,1024]{1,0:T(1,128)} %bitcast.22, f32[1,1024]{1,0:T(1,128)} %bitcast.23, f32[32,256]{1,0:T(8,128)} %params_ref.3), custom_call_target="tpu_custom_call" | custom-call | tf_op jit(solution)/shard_map/products/pallas_call | solution.py:268
  90.9 7.6 %update.1 = f32[32,256]{1,0:T(8,128)} custom-call(f32[128,128]{1,0:T(8,128)} %bitcast.21, f32[32,128]{1,0:T(8,128)} %get-tuple-element.13.cross_ref, f32[128,256]{1,0:T(8,128)} %bitcast.20, f32[32,256]{1,0:T(8,128)} %params_ref.3), custom_call_target="tpu_custom_call" | custom-call | tf_op jit(solution)/shard_map/update/pallas_call | solution.py:346
Async XLA Ops:
  2.7 39.9 %collective-permute-start = (bf16[32,64,128]{2,1,0:T(8,128)(2,1)}, bf16[32,64,128]{2,1,0:T(8,128)(2,1)S(1)}, u32[]{:S(2)}, u32[]{:S(2)}) collective-permute-start(bf16[32,64,128]{2,1,0:T(8,128)(2,1)} %get-tuple-element.19), channel_id=1, source_target_pairs={{0,1},{1,2},{2,3},{3,4},{4,5},{5,6},{6,7},{8,9},{9,10},{10,11},{11... | collective-permute-start | bytes 1572872 | tf_op jit(solution)/shard_map/ppermute | solution.py:357
  9.7 43.0 %collective-permute-start.1 = (bf16[32,64,128]{2,1,0:T(8,128)(2,1)}, bf16[32,64,128]{2,1,0:T(8,128)(2,1)S(1)}, u32[]{:S(2)}, u32[]{:S(2)}) collective-permute-start(bf16[32,64,128]{2,1,0:T(8,128)(2,1)} %get-tuple-element.17), channel_id=1, source_target_pairs={{0,1},{1,2},{2,3},{3,4},{4,5},{5,6},{6,7},{8,9},{9,10},{10,11},{11... | collective-permute-start | bytes 1572872 | tf_op jit(solution)/shard_map/ppermute | solution.py:358
  13.2 39.6 %collective-permute-start.2 = (bf16[32,64,128]{2,1,0:T(8,128)(2,1)S(1)}, bf16[32,64,128]{2,1,0:T(8,128)(2,1)S(1)}, u32[]{:S(2)}, u32[]{:S(2)}) collective-permute-start(bf16[32,64,128]{2,1,0:T(8,128)(2,1)S(1)} %get-tuple-element.18), channel_id=1, source_target_pairs={{1,0},{2,1},{3,2},{4,3},{5,4},{6,5},{7,6},{9,8},{10,9},{11,10},{12... | collective-permute-start | bytes 1572872 | tf_op jit(solution)/shard_map/ppermute | solution.py:359
  14.5 38.3 %collective-permute-start.3 = (bf16[32,64,128]{2,1,0:T(8,128)(2,1)S(1)}, bf16[32,64,128]{2,1,0:T(8,128)(2,1)S(1)}, u32[]{:S(2)}, u32[]{:S(2)}) collective-permute-start(bf16[32,64,128]{2,1,0:T(8,128)(2,1)S(1)} %get-tuple-element.16), channel_id=1, source_target_pairs={{1,0},{2,1},{3,2},{4,3},{5,4},{6,5},{7,6},{9,8},{10,9},{11,10},{12... | collective-permute-start | bytes 1572872 | tf_op jit(solution)/shard_map/ppermute | solution.py:360
  16.4 17.9 %copy-start.4 = (s32[1024]{0:T(1024)S(1)}, s32[1024]{0:T(1024)}, u32[]{:S(2)}) copy-start(s32[1024]{0:T(1024)} %param.10) | copy-start | bytes 12292
  42.7 10.1 %copy-start = (bf16[32,64,128]{2,1,0:T(8,128)(2,1)}, bf16[32,64,128]{2,1,0:T(8,128)(2,1)S(1)}, u32[]{:S(2)}) copy-start(bf16[32,64,128]{2,1,0:T(8,128)(2,1)S(1)} %collective-permute-done.ulo_ref) | copy-start | bytes 1572868
  52.8 0.8 copy-start.1
  52.8 1.0 copy-start.2
  52.8 1.2 %copy-start.3 = (bf16[32,64,128]{2,1,0:T(8,128)(2,1)}, bf16[32,64,128]{2,1,0:T(8,128)(2,1)S(1)}, u32[]{:S(2)}) copy-start(bf16[32,64,128]{2,1,0:T(8,128)(2,1)S(1)} %collective-permute-done.3.khi_ref) | copy-start | bytes 1572868
